TPU v7x, 128 devices: a whole 4x4x4 slice. The times are simulated.
128 devices in a mesh: member: 8 (over x, z_hi), space: 16 (over y, z_lo, core).
Axes of the slice: x: 4, y: 4, z: 4 (z_hi: 2, z_lo: 2; z = z_hi * 2 + z_lo), core: 2. Of those that a mesh axis runs over, the one named last changes fastest.
Arguments:
- prior_samples: float32 [256, 128, 4096], P('member', 'space'), may hold values from -6 to 6
- external_drive: float32 [128, 4096], P('space'), may hold values from -6 to 6
- obs_value: float32 [16, 32, 1024], P('space', 'member'), may hold values from -6 to 6
- obs_index: int32 [16, 32, 1024], P('space', 'member'), may hold values from 0 to 1023
- obs_weight: bfloat16 [16, 32, 1024], P('space', 'member'), may hold values from 0.5 to 8
Outputs:
- analysis: float32 [256, 128, 4096], P('member', 'space')
Inputs may be any that keep to these rules, and one draw needn't show every extreme that they name: `obs_index`: the cell is numbered row by row within the region: row times 128 plus column.
All inputs are finite; a program needn't handle non-finite values.
Results may differ from a plain program's by a relative error of at most 0.0017.
Values may be sent and summed in bfloat16 or wider, within the bound.
No kernel may reach another device: no remote copies, remote signals or barrier semaphores. Data moves between devices by JAX's collectives and lax.ppermute only.
A program may use at most 128 MiB of HBM per device.

v0:
```python
import math
from functools import partial

import jax
import jax.numpy as jnp
from jax import lax
from jax.experimental import pallas as pl
from jax.experimental.pallas import tpu as pltpu
from jax.sharding import Mesh, PartitionSpec as P

STEPS = 8
ITERS = 6
ROWS = 8
LANES = 128
PLANE = 4
F32 = jnp.float32
BF16 = jnp.bfloat16


def lane_index(rows):
    return lax.broadcasted_iota(jnp.int32, (rows, LANES), 1)


def halves(x):
    high = x.astype(BF16)
    return high, (x - high.astype(F32)).astype(BF16)


def thirds(x):
    high = x.astype(BF16)
    rest = x - high.astype(F32)
    mid = rest.astype(BF16)
    return high, mid, (rest - mid.astype(F32)).astype(BF16)


def product(a, b):
    ah, al = halves(a)
    bh, bl = halves(b)
    return jnp.dot(
        jnp.concatenate([ah, ah, al], 1),
        jnp.concatenate([bh, bl, bh], 0),
        preferred_element_type=F32,
    )


def against_rows(a, b):
    return lax.dot_general(a, b, (((1,), (1,)), ((), ())), preferred_element_type=F32)


def pack_kernel(tiles, me_ref, prior, drive, value, index, weight, chunk, extra, stage):
    lane = lane_index(16)
    groups = tiles // PLANE

    def place(tile):
        return lax.rem(tile, PLANE) * groups + tile // PLANE

    def rounding(tile, carry):
        cols = pl.ds(pl.multiple_of(tile * LANES, LANES), LANES)
        left = [jnp.zeros((16, LANES), F32)] * 2
        slot = lax.rem(tile, 2)
        stage[slot] = prior[:, cols]
        for row in range(ROWS):
            cells = jnp.concatenate(
                [stage[slot, pl.ds(row, 8, stride=8)], stage[slot, pl.ds(64 + row, 8, stride=8)]], 0
            )
            wanted = cells + left[row % 2]
            kept = wanted.astype(BF16)
            left[row % 2] = wanted - kept.astype(F32)
            chunk[place(tile), row] = kept
        return carry

    lax.fori_loop(0, tiles, rounding, 0)

    def edges(tile, carry):
        before = place(lax.rem(tile + tiles - 1, tiles))
        after = place(lax.rem(tile + 1, tiles))
        total = jnp.zeros((16, LANES), F32)
        for row in range(ROWS):
            both = jnp.where(
                lane >= LANES // 2, chunk[before, row].astype(F32), chunk[after, row].astype(F32)
            )
            moved = pltpu.roll(both, (16 * row + 8) % LANES, 1)
            total = jnp.where(lane // 16 == row, moved, total)
        chunk[place(tile), ROWS] = total.astype(BF16)
        return carry

    lax.fori_loop(0, tiles, edges, 0)

    @pl.when(pl.program_id(0) == 0)
    def _():
        lane8 = lane_index(8)
        weights = weight[0].astype(F32)
        for part in range(PLANE):
            tile = me_ref[0] * PLANE + part

            def forcing(t):
                return drive[:, pl.ds(pl.multiple_of(lax.rem(t + tiles, tiles) * LANES, LANES), LANES)]

            main = forcing(tile)
            low = pltpu.roll(jnp.where(lane8 >= LANES // 2, forcing(tile - 1), main), 8, 1)
            low = jnp.where(lane8 < 32, low, 0.0)
            high = pltpu.roll(jnp.where(lane8 < LANES // 2, forcing(tile + 1), main), 8, 1)
            high = jnp.where((lane8 < 24) | (lane8 >= 120), high, 0.0)
            low = low + pltpu.roll(low, 32, 1)
            low = low + pltpu.roll(low, 64, 1)
            high = high + pltpu.roll(high, 32, 1)
            high = high + pltpu.roll(high, 64, 1)
            extra[part, 0:1, :] = value[0, part : part + 1, :]
            extra[part, 1:2, :] = index[0, part : part + 1, :].astype(F32)
            extra[part, 2:3, :] = weights[part : part + 1, :]
            for slot, field in ((3, main), (4, low), (5, high)):
                for row in range(ROWS):
                    extra[part, slot : slot + 1, row * LANES : (row + 1) * LANES] = field[row : row + 1]
            extra[part, 6:8, :] = jnp.zeros((2, ROWS * LANES), F32)


def pack(me, prior, drive, value, index, weight):
    members, rows, cols = prior.shape
    tiles = cols // LANES
    obs = value.shape[2]
    half = members // 2
    return pl.pallas_call(
        partial(pack_kernel, tiles),
        grid_spec=pltpu.PrefetchScalarGridSpec(
            num_scalar_prefetch=1,
            grid=(2,),
            in_specs=[
                pl.BlockSpec((half * rows, cols), lambda i, s: (i, 0)),
                pl.BlockSpec((rows, cols), lambda i, s: (0, 0)),
                pl.BlockSpec((1, PLANE, obs), lambda i, s: (0, 0, 0)),
                pl.BlockSpec((1, PLANE, obs), lambda i, s: (0, 0, 0)),
                pl.BlockSpec((1, PLANE, obs), lambda i, s: (0, 0, 0)),
            ],
            out_specs=[
                pl.BlockSpec((tiles, ROWS + 1, half, LANES), lambda i, s: (0, 0, i, 0)),
                pl.BlockSpec((PLANE, 8, ROWS * LANES), lambda i, s: (0, 0, 0)),
            ],
            scratch_shapes=[pltpu.VMEM((2, half * rows, LANES), F32)],
        ),
        out_shape=[
            jax.ShapeDtypeStruct((tiles, ROWS + 1, members, LANES), BF16),
            jax.ShapeDtypeStruct((PLANE, 8, ROWS * LANES), F32),
        ],
        name="pack",
    )(me, prior.reshape(members * rows, cols), drive, value, index, weight)


def forecast_kernel(inside, cells, top, bottom, drive, drive_top, drive_bottom, out, state, force):
    depth = (PLANE + 2) * ROWS
    lane = lane_index(8)

    @pl.when(pl.program_id(0) == 0)
    def _():
        for row in range(depth):
            strip, r = divmod(row, ROWS)
            spot = slice(r * LANES, (r + 1) * LANES)
            for slot in range(3):
                pick = slice(3 + slot, 4 + slot)
                if strip == 0:
                    line = drive_top[pick, spot]
                elif strip == PLANE + 1:
                    line = drive_bottom[pick, spot]
                else:
                    line = drive[strip - 1, pick, spot]
                force[slot, row] = jnp.broadcast_to(line * 0.005, (8, LANES))

    for row in range(depth):
        strip, r = divmod(row, ROWS)
        if strip == 0:
            main, edge = top[0, r], top[0, ROWS]
        elif strip == PLANE + 1:
            main, edge = bottom[0, r], bottom[0, ROWS]
        else:
            main, edge = cells[strip - 1, 0, r], cells[strip - 1, 0, ROWS]
        main = main.astype(F32) * 0.05
        edge = edge.astype(F32) * 0.05
        low = jnp.zeros((8, LANES), F32)
        high = jnp.zeros((8, LANES), F32)
        for k in range(4):
            here = main[8 * k : 8 * k + 8]
            state[k, row] = here
            moved = pltpu.roll(here, 32 * k + 8, 1)
            beside = pltpu.roll(edge[8 * k : 8 * k + 8], (32 * k - 16 * r) % LANES, 1)
            at = (lane - 32 * k + LANES) % LANES
            low = jnp.where(at < 8, beside, jnp.where(at < 24, moved, low))
            high = jnp.where(
                (at < 8) | (at >= 120), moved, jnp.where(at < 16, beside, high)
            )
        state[4, row] = low
        state[5, row] = high

    keep_top, keep_bottom = inside[0], inside[1]

    def group(g, carry):
        kind = jnp.maximum(g - 3, 0)
        for step in range(STEPS):
            first, last = step + 1, depth - 2 - step
            above, here = state[g, first - 1], state[g, first]
            for row in range(first, last + 1):
                below = state[g, row + 1]
                east, west = pltpu.roll(here, LANES - 1, 1), pltpu.roll(here, 1, 1)
                turn = (west - east) + (above - below) + 0.05
                fresh = (
                    force[kind, row]
                    + here * turn
                    + 0.05 * (east + west)
                    + 0.4 * (above + below)
                )
                if row < ROWS:
                    fresh = fresh * keep_top
                if row >= depth - ROWS:
                    fresh = fresh * keep_bottom
                state[g, row] = fresh
                above, here = here, below
        return carry

    lax.fori_loop(0, 6, group, 0)

    outer = (lane < 8) | (lane >= LANES - 8)
    for row in range(ROWS, depth - ROWS):
        strip, r = divmod(row - ROWS, ROWS)
        both = jnp.where(lane % 32 < 8, state[5, row], state[4, row])
        for k in range(4):
            side = pltpu.roll(both, (120 - 32 * k) % LANES, 1)
            out[strip, 8 * k : 8 * k + 8, r * LANES : (r + 1) * LANES] = 20.0 * jnp.where(
                outer, side, state[k, row]
            )


def forecast(inside, cells, top, bottom, drive, drive_top, drive_bottom):
    _, groups, lines, members, _ = cells.shape
    whole = lambda shape: pl.BlockSpec(shape, lambda i: (0,) * len(shape))
    return pl.pallas_call(
        forecast_kernel,
        grid=(groups,),
        in_specs=[
            pl.BlockSpec(memory_space=pltpu.SMEM),
            pl.BlockSpec((PLANE, 1, lines, members, LANES), lambda i: (0, i, 0, 0, 0)),
            pl.BlockSpec((1, lines, members, LANES), lambda i: (i, 0, 0, 0)),
            pl.BlockSpec((1, lines, members, LANES), lambda i: (i, 0, 0, 0)),
            whole(drive.shape),
            whole(drive_top.shape),
            whole(drive_bottom.shape),
        ],
        out_specs=pl.BlockSpec((PLANE, members, ROWS * LANES), lambda i: (0, i, 0)),
        out_shape=jax.ShapeDtypeStruct((PLANE, groups * members, ROWS * LANES), F32),
        scratch_shapes=[
            pltpu.VMEM((6, (PLANE + 2) * ROWS, 8, LANES), F32),
            pltpu.VMEM((3, (PLANE + 2) * ROWS, 8, LANES), F32),
        ],
        name="forecast",
    )(inside, cells, top, bottom, drive, drive_top, drive_bottom)


def to_tile(line):
    return jnp.concatenate([line[:, r * LANES : (r + 1) * LANES] for r in range(ROWS)], 0)


def to_line(tile):
    return jnp.concatenate([tile[r : r + 1] for r in range(ROWS)], 1)


def curvature_kernel(states, obs, own, up, down):
    block = pl.program_id(0)
    blocks = pl.num_programs(0)
    members = states.shape[1]
    cells = states[0]
    centre = jnp.sum(cells, axis=0, keepdims=True) * (1.0 / members)
    anomaly = (cells - centre).astype(BF16)
    value, index, weight = obs[0, 0:1], obs[0, 1:2], obs[0, 2:3]
    row_of = jnp.floor(index * (1.0 / LANES))
    col_of = index - row_of * LANES
    count = index.shape[1]
    in_row = lax.broadcasted_iota(jnp.int32, (ROWS, count), 0).astype(F32) == row_of
    in_col = jnp.where(
        lax.broadcasted_iota(jnp.int32, (LANES, count), 0).astype(F32) == col_of, 1.0, 0.0
    ).astype(BF16)
    parts = jnp.concatenate(thirds(to_tile(centre)), 0)
    seen = jnp.dot(parts, in_col, preferred_element_type=F32)
    seen = (seen[:ROWS] + seen[ROWS : 2 * ROWS]) + seen[2 * ROWS :]
    obs_mean = jnp.sum(jnp.where(in_row, seen, 0.0), axis=0, keepdims=True)
    innovation = (value - obs_mean).astype(BF16).astype(F32)
    pull_high, pull_low = halves(weight * innovation)
    spread = jnp.concatenate(
        [
            jnp.where(in_row, weight, 0.0),
            jnp.where(in_row, pull_high.astype(F32), 0.0),
            jnp.where(in_row, pull_low.astype(F32), 0.0),
        ],
        0,
    ).astype(BF16)
    summed = against_rows(spread, in_col)
    weights = summed[:ROWS]
    pulls = summed[ROWS : 2 * ROWS] + summed[2 * ROWS :]
    row_pos = lax.broadcasted_iota(jnp.int32, (ROWS, LANES), 0).astype(F32)
    span = float(ROWS)
    fall_down = jnp.exp(-2.0 * (span - row_pos) * (span - row_pos) / (span * span))
    fall_up = jnp.exp(-2.0 * (row_pos + 1.0) * (row_pos + 1.0) / (span * span))
    wide = anomaly.astype(F32)
    ones = jnp.ones((ROWS, LANES), F32)
    factors = (ones, fall_up, fall_down)
    terms = [
        against_rows((wide * to_line(weights * f)).astype(BF16), anomaly) for f in factors
    ]
    lines = []
    for f in factors:
        lines.extend(thirds(to_line(pulls * f)))
    lines.append(jnp.zeros((7, count), BF16))
    vectors = against_rows(jnp.concatenate(lines, 0), anomaly)
    sides = [
        (vectors[3 * i : 3 * i + 1] + vectors[3 * i + 1 : 3 * i + 2]) + vectors[3 * i + 2 : 3 * i + 3]
        for i in range(3)
    ]
    pad = jnp.zeros((7, members), F32)

    @pl.when(block == 0)
    def _():
        own[...] = jnp.zeros_like(own)
        up[:members] = terms[1]
        up[members:] = jnp.concatenate([sides[1], pad], 0)

    own[block, :members] += terms[0]
    own[block, members:] += jnp.concatenate([sides[0], pad], 0)

    @pl.when(block > 0)
    def _():
        own[block - 1, :members] += terms[1]
        own[block - 1, members:] += jnp.concatenate([sides[1], pad], 0)

    @pl.when(block < blocks - 1)
    def _():
        own[block + 1, :members] += terms[2]
        own[block + 1, members:] += jnp.concatenate([sides[2], pad], 0)

    @pl.when(block == blocks - 1)
    def _():
        down[:members] = terms[2]
        down[members:] = jnp.concatenate([sides[2], pad], 0)


def curvatures(states, obs):
    blocks, members, width = states.shape
    whole = lambda shape: pl.BlockSpec(shape, lambda i: (0,) * len(shape))
    return pl.pallas_call(
        curvature_kernel,
        grid=(blocks,),
        in_specs=[
            pl.BlockSpec((1, members, width), lambda i: (i, 0, 0)),
            pl.BlockSpec((1, 8, width), lambda i: (i, 0, 0)),
        ],
        out_specs=[
            whole((blocks, members + 8, members)),
            whole((members + 8, members)),
            whole((members + 8, members)),
        ],
        out_shape=[
            jax.ShapeDtypeStruct((blocks, members + 8, members), F32),
            jax.ShapeDtypeStruct((members + 8, members), F32),
            jax.ShapeDtypeStruct((members + 8, members), F32),
        ],
        name="curvature",
    )(states, obs)


def transform_kernel(own, from_above, from_below, out, iterate, inverse):
    blocks, size, _ = iterate.shape
    row = lax.broadcasted_iota(jnp.int32, (size, size), 0)
    col = lax.broadcasted_iota(jnp.int32, (size, size), 1)
    diagonal = row == col

    def middle_of(x):
        return jnp.where(diagonal, 1.5 - 0.5 * x, -0.5 * x)

    norms, sides = [], []
    for b in range(blocks):
        matrix, side = own[b, :size], own[b, size:]
        if b == 0:
            matrix, side = matrix + from_above[:size], side + from_above[size:]
        if b == blocks - 1:
            matrix, side = matrix + from_below[:size], side + from_below[size:]
        matrix = matrix + jnp.where(diagonal, size - 1.0, 0.0)
        squares = jnp.sum(jnp.sum(matrix * matrix, axis=0, keepdims=True), axis=1, keepdims=True)
        norm = jnp.sqrt(squares)
        start = matrix / norm
        middle = middle_of(start)
        inverse[b] = middle
        iterate[b] = product(start, middle)
        norms.append(norm)
        sides.append(side)

    def sweep(i, carry):
        middles = [middle_of(product(inverse[b], iterate[b])) for b in range(blocks)]
        for b in range(blocks):
            both = product(jnp.concatenate([iterate[b], inverse[b]], 0), middles[b])
            iterate[b] = both[:size]
            inverse[b] = both[size:]
        return carry

    lax.fori_loop(0, ITERS - 2, sweep, 0)
    middles = [middle_of(product(inverse[b], iterate[b])) for b in range(blocks)]
    finals = [product(inverse[b], middles[b]) for b in range(blocks)]
    for b in range(blocks):
        flipped = finals[b].T
        inner = product(sides[b], flipped)
        shift = product(inner, flipped) / norms[b]
        out[b, :size] = flipped * (math.sqrt(size - 1.0) / jnp.sqrt(norms[b]))
        out[b, size:] = shift


def transforms(own, from_above, from_below):
    blocks, _, size = own.shape
    return pl.pallas_call(
        transform_kernel,
        out_shape=jax.ShapeDtypeStruct(own.shape, F32),
        scratch_shapes=[
            pltpu.VMEM((blocks, size, size), F32),
            pltpu.VMEM((blocks, size, size), F32),
        ],
        name="transform",
    )(own, from_above, from_below)


def apply_kernel(share, states, weights, out):
    members = states.shape[1]
    cells = states[0]
    centre = jnp.sum(cells, axis=0, keepdims=True) * (1.0 / members)
    moved = product(weights[0], cells - centre)
    common_high, common_low = halves(centre + moved[members : members + 1])
    common = jnp.concatenate(
        [to_tile(common_high.astype(F32)), to_tile(common_low.astype(F32))], 0
    ).astype(BF16)
    for part in range(members // share):
        for r in range(ROWS):
            out[0, part, r * share : (r + 1) * share] = moved[
                part * share : (part + 1) * share, r * LANES : (r + 1) * LANES
            ].astype(BF16)
        out[0, part, ROWS * share :] = common


def apply_transform(share, states, weights):
    blocks, members, width = states.shape
    lines = ROWS * share + 16
    return pl.pallas_call(
        partial(apply_kernel, share),
        grid=(blocks,),
        in_specs=[
            pl.BlockSpec((1, members, width), lambda i: (i, 0, 0)),
            pl.BlockSpec((1, members + 8, members), lambda i: (i, 0, 0)),
        ],
        out_specs=pl.BlockSpec((1, members // share, lines, LANES), lambda i: (i, 0, 0, 0)),
        out_shape=jax.ShapeDtypeStruct((blocks, members // share, lines, LANES), BF16),
        name="apply",
    )(states, weights)


def unpack_kernel(share, chunk, out, stage):
    for part in range(PLANE):
        cols = slice(part * LANES, (part + 1) * LANES)
        common = chunk[part, 0, ROWS * share :].astype(F32)
        common = common[:ROWS] + common[ROWS:]
        for r in range(ROWS):
            field = chunk[part, 0, r * share : (r + 1) * share].astype(F32) + common[r : r + 1]
            for k in range(share // 8):
                stage[part, pl.ds(64 * k + r, 8, stride=8)] = field[8 * k : 8 * k + 8]
        out[:, cols] = stage[part]


def unpack(share, chunk):
    _, groups, lines, _ = chunk.shape
    return pl.pallas_call(
        partial(unpack_kernel, share),
        grid=(groups,),
        in_specs=[pl.BlockSpec((PLANE, 1, lines, LANES), lambda i: (0, i, 0, 0))],
        out_specs=pl.BlockSpec((share * ROWS, PLANE * LANES), lambda i: (0, i)),
        out_shape=jax.ShapeDtypeStruct((share * ROWS, groups * PLANE * LANES), F32),
        scratch_shapes=[pltpu.VMEM((PLANE, share * ROWS, LANES), F32)],
        name="unpack",
    )(chunk)


def local(prior, drive, value, index, weight):
    members, rows, cols = prior.shape
    groups = lax.axis_size("member")
    planes = lax.axis_size("y")
    plane = lax.axis_index("y")
    upward = [(i + 1, i) for i in range(planes - 1)]
    downward = [(i, i + 1) for i in range(planes - 1)]
    me = lax.axis_index("member").reshape(1).astype(jnp.int32)
    chunk, extra = pack(me, prior, drive, value, index, weight)
    extra = lax.all_to_all(extra, "zc", 0, 0, tiled=True)
    chunk = lax.all_to_all(chunk, ("zc", "member"), 0, 0, tiled=True)
    cells = chunk.reshape(PLANE, groups, ROWS + 1, members, LANES)
    bottom = lax.ppermute(cells[0], "y", upward)
    top = lax.ppermute(cells[PLANE - 1], "y", downward)
    drive_bottom = lax.ppermute(extra[0], "y", upward)
    drive_top = lax.ppermute(extra[PLANE - 1], "y", downward)
    inside = jnp.stack([plane > 0, plane < planes - 1]).astype(F32)
    states = forecast(inside, cells, top, bottom, extra, drive_top, drive_bottom)
    own, up, down = curvatures(states, extra)
    from_below = lax.ppermute(up, "y", upward)
    from_above = lax.ppermute(down, "y", downward)
    weights = transforms(own, from_above, from_below)
    analysed = apply_transform(members, states, weights)
    lines = ROWS * members + 16
    back = lax.all_to_all(
        analysed.reshape(PLANE * groups, lines, LANES), ("zc", "member"), 0, 0, tiled=True
    )
    return unpack(members, back.reshape(PLANE, groups, lines, LANES)).reshape(members, rows, cols)


def solution(mesh):
    groups, spaces = mesh.devices.shape
    fine = Mesh(mesh.devices.reshape(groups, spaces // PLANE, PLANE), ("member", "y", "zc"))
    rows = ("y", "zc")
    return jax.shard_map(
        local,
        mesh=fine,
        in_specs=(
            P("member", rows, None),
            P(rows, None),
            P(rows, "member", None),
            P(rows, "member", None),
            P(rows, "member", None),
        ),
        out_specs=P("member", rows, None),
        check_vma=False,
    )
```

profile of v0, /device:TPU:1, one launch (start us, length us, event | category | flops | bytes accessed | tf_op | source)
XLA Modules:
  0.0 197.4 jit_solution(17281181951817121934)
XLA Ops:
  0.0 10.3 %pack.1 = (bf16[32,9,32,128]{3,2,1,0:T(8,128)(2,1)}, f32[4,8,1024]{2,1,0:T(8,128)}) custom-call(s32[1]{0:T(128)} %bitcast.2.me_ref, f32[256,4096]{1,0:T(8,128)} %bitcast.15, f32[8,4096]{1,0:T(8,128)} %drive.1, f32[1,4,1024]{2,1,0:T(4,128)} %value.1, s32[1,4,1024]{2,1,0:T(4,128)} %index.1, bf16[1,4,1024]{2,1,0:T(4,128)(2,1)} %weight.1), custom_call_target="tpu_custom_call" | custom-call | tf_op jit(solution)/shard_map/pack/pallas_call | solution.py:122
  10.3 41.0 %all_to_all.15 = bf16[32,9,32,128]{3,2,1,0:T(8,128)(2,1)S(1)} all-to-all(bf16[32,9,32,128]{3,2,1,0:T(8,128)(2,1)} %get-tuple-element.10), channel_id=1, replica_groups=mesh['member'=8,'y'=4,'zc'=4] {'zc','member'}, dimensions={0} | all-to-all | bytes 4718592 | tf_op jit(solution)/shard_map/all_to_all | solution.py:491
  51.3 0.0 copy-start
  51.3 1.4 fusion
  52.7 1.3 collective-permute-start.1
  54.0 4.8 %collective-permute-start = (bf16[8,9,32,128]{3,2,1,0:T(8,128)(2,1)}, bf16[8,9,32,128]{3,2,1,0:T(8,128)(2,1)}, u32[]{:S(2)}, u32[]{:S(2)}) collective-permute-start(bf16[8,9,32,128]{3,2,1,0:T(8,128)(2,1)} %get-tuple-element.16), channel_id=1, source_target_pairs={{0,4},{4,8},{8,12},{1,5},{5,9},{9,13},{2,6},{6,10},{10,14},{3,7},{... | collective-permute-start | bytes 1769480 | tf_op jit(solution)/shard_map/ppermute | solution.py:494
  58.8 3.8 %all-to-all-start.1 = ((f32[4,8,1024]{2,1,0:T(8,128)}), f32[4,8,1024]{2,1,0:T(8,128)S(1)}, u32[]{:S(2)}, u32[]{:S(2)}) async-start(f32[4,8,1024]{2,1,0:T(8,128)} %get-tuple-element.11), calls=%async_computation.1 | async-start | bytes 262144 | tf_op jit(solution)/shard_map/all_to_all | solution.py:490
  62.6 3.9 %all-to-all-done.1.drive.obs = f32[4,8,1024]{2,1,0:T(8,128)S(1)} async-done(((f32[4,8,1024]{2,1,0:T(8,128)}), f32[4,8,1024]{2,1,0:T(8,128)S(1)}, u32[]{:S(2)}, u32[]{:S(2)}) %all-to-all-start.1) | async-done | bytes 131104 | tf_op jit(solution)/shard_map/all_to_all | solution.py:490
  66.5 0.0 copy-start.1
  66.5 1.3 collective-permute-start.3
  67.8 4.0 %collective-permute-start.2 = (f32[8,1024]{1,0:T(8,128)S(1)}, f32[8,1024]{1,0:T(8,128)S(1)}, u32[]{:S(2)}, u32[]{:S(2)}) collective-permute-start(f32[8,1024]{1,0:T(8,128)S(1)} %get-tuple-element.18), channel_id=1, source_target_pairs={{0,4},{4,8},{8,12},{1,5},{5,9},{9,13},{2,6},{6,10},{10,14},{3,7},{... | collective-permute-start | bytes 98312 | tf_op jit(solution)/shard_map/ppermute | solution.py:496
  71.8 0.6 add_convert_fusion.inside
  72.4 0.0 collective-permute-done.3.drive_bottom
  72.4 0.0 copy-start.5
  72.4 0.4 collective-permute-done.2.drive_top
  72.8 0.0 copy-start.6
  72.8 0.0 collective-permute-done.1.bottom
  72.8 0.0 copy-start.2
  72.8 0.0 collective-permute-done.top
  72.8 0.0 copy-done
  72.8 0.0 copy-done.1
  72.8 0.2 copy-done.5
  73.1 0.4 copy-done.6
  73.4 0.2 copy-done.2
  73.6 43.1 %forecast.1.states = f32[4,256,1024]{2,1,0:T(8,128)} custom-call(f32[2]{0:T(128)} %add_convert_fusion.inside, bf16[4,8,9,32,128]{4,3,2,1,0:T(8,128)(2,1)} %bitcast.12, bf16[8,9,32,128]{3,2,1,0:T(8,128)(2,1)} %collective-permute-done.top, bf16[8,9,32,128]{3,2,1,0:T(8,128)(2,1)} %copy-done.2, f32[4,8,1024]{2,1,0:T(8,128)} %copy-done.1, f32[8,1024]{1,0:T(8,128)} %copy-done.6, ...), custom_call_target="tpu_custom_call" | custom-call | tf_op jit(solution)/shard_map/forecast/pallas_call | solution.py:233
  116.7 7.6 %curvature.1 = (f32[4,264,256]{2,1,0:T(8,128)}, f32[264,256]{1,0:T(8,128)}, f32[264,256]{1,0:T(8,128)}) custom-call(f32[4,256,1024]{2,1,0:T(8,128)} %forecast.1.states, f32[4,8,1024]{2,1,0:T(8,128)} %copy-done.1), custom_call_target="tpu_custom_call" | custom-call | tf_op jit(solution)/shard_map/curvature/pallas_call | solution.py:344
  124.3 3.7 %collective-permute-start.4 = (f32[264,256]{1,0:T(8,128)}, f32[264,256]{1,0:T(8,128)S(1)}, u32[]{:S(2)}, u32[]{:S(2)}) collective-permute-start(f32[264,256]{1,0:T(8,128)} %get-tuple-element.13), channel_id=1, source_target_pairs={{0,4},{4,8},{8,12},{1,5},{5,9},{9,13},{2,6},{6,10},{10,14},{3,7},{... | collective-permute-start | bytes 811016 | tf_op jit(solution)/shard_map/ppermute | solution.py:501
  127.9 1.3 collective-permute-start.5
  129.2 2.6 %collective-permute-done.4.from_above = f32[264,256]{1,0:T(8,128)S(1)} collective-permute-done((f32[264,256]{1,0:T(8,128)}, f32[264,256]{1,0:T(8,128)S(1)}, u32[]{:S(2)}, u32[]{:S(2)}) %collective-permute-start.4) | collective-permute-done | bytes 270368 | tf_op jit(solution)/shard_map/ppermute | solution.py:501
  131.9 0.0 copy-start.3
  131.9 3.5 %collective-permute-done.5.from_below = f32[264,256]{1,0:T(8,128)S(1)} collective-permute-done((f32[264,256]{1,0:T(8,128)}, f32[264,256]{1,0:T(8,128)S(1)}, u32[]{:S(2)}, u32[]{:S(2)}) %collective-permute-start.5) | collective-permute-done | bytes 270368 | tf_op jit(solution)/shard_map/ppermute | solution.py:500
  135.3 0.0 copy-start.4
  135.3 0.0 copy-done.3
  135.3 0.7 copy-done.4
  136.1 10.6 %transform.1.weights = f32[4,264,256]{2,1,0:T(8,128)} custom-call(f32[4,264,256]{2,1,0:T(8,128)} %get-tuple-element.12.own, f32[264,256]{1,0:T(8,128)} %copy-done.3, f32[264,256]{1,0:T(8,128)} %copy-done.4), custom_call_target="tpu_custom_call" | custom-call | tf_op jit(solution)/shard_map/transform/pallas_call | solution.py:412
  146.6 5.8 %apply.1 = bf16[4,8,272,128]{3,2,1,0:T(8,128)(2,1)} custom-call(f32[4,256,1024]{2,1,0:T(8,128)} %forecast.1.states, f32[4,264,256]{2,1,0:T(8,128)} %transform.1.weights), custom_call_target="tpu_custom_call" | custom-call | tf_op jit(solution)/shard_map/apply/pallas_call | solution.py:443
  152.4 38.4 %all_to_all.16 = bf16[32,272,128]{2,1,0:T(8,128)(2,1)} all-to-all(bf16[32,272,128]{2,1,0:T(8,128)(2,1)} %bitcast.13), channel_id=1, replica_groups=mesh['member'=8,'y'=4,'zc'=4] {'zc','member'}, dimensions={0} | all-to-all | bytes 4456448 | tf_op jit(solution)/shard_map/all_to_all | solution.py:505
  190.8 6.6 %unpack.1 = f32[256,4096]{1,0:T(8,128)} custom-call(bf16[4,8,272,128]{3,2,1,0:T(8,128)(2,1)} %bitcast.14), custom_call_target="tpu_custom_call" | custom-call | tf_op jit(solution)/shard_map/unpack/pallas_call | solution.py:470
  (1 shorter events, 0.0 us)
Async XLA Ops:
  51.3 21.5 %copy-start = (bf16[32,9,32,128]{3,2,1,0:T(8,128)(2,1)}, bf16[32,9,32,128]{3,2,1,0:T(8,128)(2,1)S(1)}, u32[]{:S(2)}) copy-start(bf16[32,9,32,128]{3,2,1,0:T(8,128)(2,1)S(1)} %all_to_all.15) | copy-start | bytes 7077892
  52.7 20.1 %collective-permute-start.1 = (bf16[8,9,32,128]{3,2,1,0:T(8,128)(2,1)}, bf16[8,9,32,128]{3,2,1,0:T(8,128)(2,1)S(1)}, u32[]{:S(2)}, u32[]{:S(2)}) collective-permute-start(bf16[8,9,32,128]{3,2,1,0:T(8,128)(2,1)} %get-tuple-element.15), channel_id=1, source_target_pairs={{4,0},{8,4},{12,8},{5,1},{9,5},{13,9},{6,2},{10,6},{14,10},{7,3},{... | collective-permute-start | bytes 1769480 | tf_op jit(solution)/shard_map/ppermute | solution.py:493
  54.0 18.9 %collective-permute-start = (bf16[8,9,32,128]{3,2,1,0:T(8,128)(2,1)}, bf16[8,9,32,128]{3,2,1,0:T(8,128)(2,1)}, u32[]{:S(2)}, u32[]{:S(2)}) collective-permute-start(bf16[8,9,32,128]{3,2,1,0:T(8,128)(2,1)} %get-tuple-element.16), channel_id=1, source_target_pairs={{0,4},{4,8},{8,12},{1,5},{5,9},{9,13},{2,6},{6,10},{10,14},{3,7},{... | collective-permute-start | bytes 1769480 | tf_op jit(solution)/shard_map/ppermute | solution.py:494
  58.8 7.7 %all-to-all-start.1 = ((f32[4,8,1024]{2,1,0:T(8,128)}), f32[4,8,1024]{2,1,0:T(8,128)S(1)}, u32[]{:S(2)}, u32[]{:S(2)}) async-start(f32[4,8,1024]{2,1,0:T(8,128)} %get-tuple-element.11), calls=%async_computation.1 | async-start | bytes 262144 | tf_op jit(solution)/shard_map/all_to_all | solution.py:490
  66.5 6.3 %copy-start.1 = (f32[4,8,1024]{2,1,0:T(8,128)}, f32[4,8,1024]{2,1,0:T(8,128)S(1)}, u32[]{:S(2)}) copy-start(f32[4,8,1024]{2,1,0:T(8,128)S(1)} %all-to-all-done.1.drive.obs) | copy-start | bytes 393220
  66.5 5.9 %collective-permute-start.3 = (f32[8,1024]{1,0:T(8,128)S(1)}, f32[8,1024]{1,0:T(8,128)S(1)}, u32[]{:S(2)}, u32[]{:S(2)}) collective-permute-start(f32[8,1024]{1,0:T(8,128)S(1)} %get-tuple-element.17), channel_id=1, source_target_pairs={{4,0},{8,4},{12,8},{5,1},{9,5},{13,9},{6,2},{10,6},{14,10},{7,3},{... | collective-permute-start | bytes 98312 | tf_op jit(solution)/shard_map/ppermute | solution.py:495
  67.8 5.0 %collective-permute-start.2 = (f32[8,1024]{1,0:T(8,128)S(1)}, f32[8,1024]{1,0:T(8,128)S(1)}, u32[]{:S(2)}, u32[]{:S(2)}) collective-permute-start(f32[8,1024]{1,0:T(8,128)S(1)} %get-tuple-element.18), channel_id=1, source_target_pairs={{0,4},{4,8},{8,12},{1,5},{5,9},{9,13},{2,6},{6,10},{10,14},{3,7},{... | collective-permute-start | bytes 98312 | tf_op jit(solution)/shard_map/ppermute | solution.py:496
  72.4 0.6 copy-start.5
  72.8 0.6 copy-start.6
  72.8 0.8 copy-start.2
  124.3 7.6 %collective-permute-start.4 = (f32[264,256]{1,0:T(8,128)}, f32[264,256]{1,0:T(8,128)S(1)}, u32[]{:S(2)}, u32[]{:S(2)}) collective-permute-start(f32[264,256]{1,0:T(8,128)} %get-tuple-element.13), channel_id=1, source_target_pairs={{0,4},{4,8},{8,12},{1,5},{5,9},{9,13},{2,6},{6,10},{10,14},{3,7},{... | collective-permute-start | bytes 811016 | tf_op jit(solution)/shard_map/ppermute | solution.py:501
  127.9 7.4 %collective-permute-start.5 = (f32[264,256]{1,0:T(8,128)}, f32[264,256]{1,0:T(8,128)S(1)}, u32[]{:S(2)}, u32[]{:S(2)}) collective-permute-start(f32[264,256]{1,0:T(8,128)} %get-tuple-element.14), channel_id=1, source_target_pairs={{4,0},{8,4},{12,8},{5,1},{9,5},{13,9},{6,2},{10,6},{14,10},{7,3},{... | collective-permute-start | bytes 811016 | tf_op jit(solution)/shard_map/ppermute | solution.py:500
  131.9 3.5 %copy-start.3 = (f32[264,256]{1,0:T(8,128)}, f32[264,256]{1,0:T(8,128)S(1)}, u32[]{:S(2)}) copy-start(f32[264,256]{1,0:T(8,128)S(1)} %collective-permute-done.4.from_above) | copy-start | bytes 811012
  135.3 0.7 copy-start.4
where the time goes:
time: 198 us; the launch traced here: 197 us
  Pallas kernels  83.9 us (42%)
  blocking collectives  79.4 us (40%)
  starting transfers between devices  20.2 us (10%)
  waiting for transfers between devices  10.3 us (5%)
  local copies, waits for them, and re-layouts  2.91 us (1%)
    pallas_call x1, Pallas kernels, forecast(): pl.pallas_call(forecast_kernel, grid=(groups,), in_specs=[pl.BlockSpec(me...  43.1 us
    all_to_all x1, blocking collectives, local(): chunk = lax.all_to_all(chunk, ('zc', 'member'), 0, 0, tiled=True)  41 us
    all_to_all x1, blocking collectives, local(): lax.all_to_all(analysed.reshape(PLANE * groups, lines, LANES), ('zc', 'me...  38.4 us
    pallas_call x1, Pallas kernels, transforms(): pl.pallas_call(transform_kernel, out_shape=jax.ShapeDtypeStruct(own.shape...  10.6 us
    pallas_call x1, Pallas kernels, pack(): pl.pallas_call(partial(pack_kernel, tiles), grid_spec=pltpu.PrefetchScala...  10.3 us
    pallas_call x1, Pallas kernels, curvatures(): pl.pallas_call(curvature_kernel, grid=(blocks,), in_specs=[pl.BlockSpec((...  7.57 us
    pallas_call x1, Pallas kernels, unpack(): pl.pallas_call(partial(unpack_kernel, share), grid=(groups,), in_specs=[p...  6.57 us
    pallas_call x1, Pallas kernels, apply_transform(): pl.pallas_call(partial(apply_kernel, share), grid=(blocks,), in_specs=[pl...  5.81 us
  transfers between devices with their start and end apart: 7, of which 4 were waited for; matrix products, arithmetic and copies ran while one was open for 0% of the time, Pallas kernels for 0%

commit v1 on v0

--- a/solution.py
+++ b/solution.py
@@ -47,7 +47,7 @@
     return lax.dot_general(a, b, (((1,), (1,)), ((), ())), preferred_element_type=F32)
 
 
-def pack_kernel(tiles, me_ref, prior, drive, value, index, weight, chunk, extra, stage):
+def pack_kernel(tiles, prior, chunk, stage):
     lane = lane_index(16)
     groups = tiles // PLANE
 
@@ -86,63 +86,57 @@
 
     lax.fori_loop(0, tiles, edges, 0)
 
-    @pl.when(pl.program_id(0) == 0)
-    def _():
-        lane8 = lane_index(8)
-        weights = weight[0].astype(F32)
-        for part in range(PLANE):
-            tile = me_ref[0] * PLANE + part
-
-            def forcing(t):
-                return drive[:, pl.ds(pl.multiple_of(lax.rem(t + tiles, tiles) * LANES, LANES), LANES)]
-
-            main = forcing(tile)
-            low = pltpu.roll(jnp.where(lane8 >= LANES // 2, forcing(tile - 1), main), 8, 1)
-            low = jnp.where(lane8 < 32, low, 0.0)
-            high = pltpu.roll(jnp.where(lane8 < LANES // 2, forcing(tile + 1), main), 8, 1)
-            high = jnp.where((lane8 < 24) | (lane8 >= 120), high, 0.0)
-            low = low + pltpu.roll(low, 32, 1)
-            low = low + pltpu.roll(low, 64, 1)
-            high = high + pltpu.roll(high, 32, 1)
-            high = high + pltpu.roll(high, 64, 1)
-            extra[part, 0:1, :] = value[0, part : part + 1, :]
-            extra[part, 1:2, :] = index[0, part : part + 1, :].astype(F32)
-            extra[part, 2:3, :] = weights[part : part + 1, :]
-            for slot, field in ((3, main), (4, low), (5, high)):
-                for row in range(ROWS):
-                    extra[part, slot : slot + 1, row * LANES : (row + 1) * LANES] = field[row : row + 1]
-            extra[part, 6:8, :] = jnp.zeros((2, ROWS * LANES), F32)
-
-
-def pack(me, prior, drive, value, index, weight):
+
+def extra_kernel(tiles, me_ref, drive, value, index, weight, extra):
+    lane8 = lane_index(8)
+    weights = weight[0].astype(F32)
+    for part in range(PLANE):
+        tile = me_ref[0] * PLANE + part
+
+        def forcing(t):
+            return drive[:, pl.ds(pl.multiple_of(lax.rem(t + tiles, tiles) * LANES, LANES), LANES)]
+
+        main = forcing(tile)
+        low = pltpu.roll(jnp.where(lane8 >= LANES // 2, forcing(tile - 1), main), 8, 1)
+        low = jnp.where(lane8 < 32, low, 0.0)
+        high = pltpu.roll(jnp.where(lane8 < LANES // 2, forcing(tile + 1), main), 8, 1)
+        high = jnp.where((lane8 < 24) | (lane8 >= 120), high, 0.0)
+        low = low + pltpu.roll(low, 32, 1)
+        low = low + pltpu.roll(low, 64, 1)
+        high = high + pltpu.roll(high, 32, 1)
+        high = high + pltpu.roll(high, 64, 1)
+        extra[part, 0:1, :] = value[0, part : part + 1, :]
+        extra[part, 1:2, :] = index[0, part : part + 1, :].astype(F32)
+        extra[part, 2:3, :] = weights[part : part + 1, :]
+        for slot, field in ((3, main), (4, low), (5, high)):
+            for row in range(ROWS):
+                extra[part, slot : slot + 1, row * LANES : (row + 1) * LANES] = field[row : row + 1]
+        extra[part, 6:8, :] = jnp.zeros((2, ROWS * LANES), F32)
+
+
+def pack_extra(me, cols, drive, value, index, weight):
+    return pl.pallas_call(
+        partial(extra_kernel, cols // LANES),
+        in_specs=[pl.BlockSpec(memory_space=pltpu.SMEM)]
+        + [pl.BlockSpec(memory_space=pltpu.VMEM)] * 4,
+        out_shape=jax.ShapeDtypeStruct((PLANE, 8, ROWS * LANES), F32),
+        name="pack_extra",
+    )(me, drive, value, index, weight)
+
+
+def pack(prior, half):
     members, rows, cols = prior.shape
     tiles = cols // LANES
-    obs = value.shape[2]
-    half = members // 2
+    part = members // 2
     return pl.pallas_call(
         partial(pack_kernel, tiles),
-        grid_spec=pltpu.PrefetchScalarGridSpec(
-            num_scalar_prefetch=1,
-            grid=(2,),
-            in_specs=[
-                pl.BlockSpec((half * rows, cols), lambda i, s: (i, 0)),
-                pl.BlockSpec((rows, cols), lambda i, s: (0, 0)),
-                pl.BlockSpec((1, PLANE, obs), lambda i, s: (0, 0, 0)),
-                pl.BlockSpec((1, PLANE, obs), lambda i, s: (0, 0, 0)),
-                pl.BlockSpec((1, PLANE, obs), lambda i, s: (0, 0, 0)),
-            ],
-            out_specs=[
-                pl.BlockSpec((tiles, ROWS + 1, half, LANES), lambda i, s: (0, 0, i, 0)),
-                pl.BlockSpec((PLANE, 8, ROWS * LANES), lambda i, s: (0, 0, 0)),
-            ],
-            scratch_shapes=[pltpu.VMEM((2, half * rows, LANES), F32)],
-        ),
-        out_shape=[
-            jax.ShapeDtypeStruct((tiles, ROWS + 1, members, LANES), BF16),
-            jax.ShapeDtypeStruct((PLANE, 8, ROWS * LANES), F32),
-        ],
+        grid=(1,),
+        in_specs=[pl.BlockSpec((part * rows, cols), lambda i: (half, 0))],
+        out_specs=pl.BlockSpec((tiles, ROWS + 1, part, LANES), lambda i: (0, 0, 0, 0)),
+        out_shape=jax.ShapeDtypeStruct((tiles, ROWS + 1, part, LANES), BF16),
+        scratch_shapes=[pltpu.VMEM((2, part * rows, LANES), F32)],
         name="pack",
-    )(me, prior.reshape(members * rows, cols), drive, value, index, weight)
+    )(prior.reshape(members * rows, cols))
 
 
 def forecast_kernel(inside, cells, top, bottom, drive, drive_top, drive_bottom, out, state, force):
@@ -167,13 +161,13 @@
     for row in range(depth):
         strip, r = divmod(row, ROWS)
         if strip == 0:
-            main, edge = top[0, r], top[0, ROWS]
+            source = top
         elif strip == PLANE + 1:
-            main, edge = bottom[0, r], bottom[0, ROWS]
+            source = bottom
         else:
-            main, edge = cells[strip - 1, 0, r], cells[strip - 1, 0, ROWS]
-        main = main.astype(F32) * 0.05
-        edge = edge.astype(F32) * 0.05
+            source = cells.at[strip - 1]
+        main = jnp.concatenate([source[0, r], source[1, r]], 0).astype(F32) * 0.05
+        edge = jnp.concatenate([source[0, ROWS], source[1, ROWS]], 0).astype(F32) * 0.05
         low = jnp.zeros((8, LANES), F32)
         high = jnp.zeros((8, LANES), F32)
         for k in range(4):
@@ -227,23 +221,24 @@
             )
 
 
-def forecast(inside, cells, top, bottom, drive, drive_top, drive_bottom):
-    _, groups, lines, members, _ = cells.shape
+def forecast(inside, cells, top, bottom, drive, drive_top, drive_bottom, begin, end):
+    _, _, lines, members, _ = cells.shape
+    at = begin // 2
     whole = lambda shape: pl.BlockSpec(shape, lambda i: (0,) * len(shape))
     return pl.pallas_call(
         forecast_kernel,
-        grid=(groups,),
+        grid=((end - begin) // 2,),
         in_specs=[
             pl.BlockSpec(memory_space=pltpu.SMEM),
-            pl.BlockSpec((PLANE, 1, lines, members, LANES), lambda i: (0, i, 0, 0, 0)),
-            pl.BlockSpec((1, lines, members, LANES), lambda i: (i, 0, 0, 0)),
-            pl.BlockSpec((1, lines, members, LANES), lambda i: (i, 0, 0, 0)),
+            pl.BlockSpec((PLANE, 2, lines, members, LANES), lambda i: (0, i + at, 0, 0, 0)),
+            pl.BlockSpec((2, lines, members, LANES), lambda i: (i + at, 0, 0, 0)),
+            pl.BlockSpec((2, lines, members, LANES), lambda i: (i + at, 0, 0, 0)),
             whole(drive.shape),
             whole(drive_top.shape),
             whole(drive_bottom.shape),
         ],
-        out_specs=pl.BlockSpec((PLANE, members, ROWS * LANES), lambda i: (0, i, 0)),
-        out_shape=jax.ShapeDtypeStruct((PLANE, groups * members, ROWS * LANES), F32),
+        out_specs=pl.BlockSpec((PLANE, 2 * members, ROWS * LANES), lambda i: (0, i, 0)),
+        out_shape=jax.ShapeDtypeStruct((PLANE, (end - begin) * members, ROWS * LANES), F32),
         scratch_shapes=[
             pltpu.VMEM((6, (PLANE + 2) * ROWS, 8, LANES), F32),
             pltpu.VMEM((3, (PLANE + 2) * ROWS, 8, LANES), F32),
@@ -260,11 +255,12 @@
     return jnp.concatenate([tile[r : r + 1] for r in range(ROWS)], 1)
 
 
-def curvature_kernel(states, obs, own, up, down):
+def curvature_kernel(pieces, *refs):
+    states, (obs, own, up, down) = refs[:pieces], refs[pieces:]
     block = pl.program_id(0)
     blocks = pl.num_programs(0)
-    members = states.shape[1]
-    cells = states[0]
+    cells = jnp.concatenate([piece[0] for piece in states], 0)
+    members = cells.shape[0]
     centre = jnp.sum(cells, axis=0, keepdims=True) * (1.0 / members)
     anomaly = (cells - centre).astype(BF16)
     value, index, weight = obs[0, 0:1], obs[0, 1:2], obs[0, 2:3]
@@ -338,16 +334,18 @@
         down[members:] = jnp.concatenate([sides[2], pad], 0)
 
 
+def of_block(states):
+    return [pl.BlockSpec((1, *piece.shape[1:]), lambda i: (i, 0, 0)) for piece in states]
+
+
 def curvatures(states, obs):
-    blocks, members, width = states.shape
+    blocks, _, width = states[0].shape
+    members = sum(piece.shape[1] for piece in states)
     whole = lambda shape: pl.BlockSpec(shape, lambda i: (0,) * len(shape))
     return pl.pallas_call(
-        curvature_kernel,
+        partial(curvature_kernel, len(states)),
         grid=(blocks,),
-        in_specs=[
-            pl.BlockSpec((1, members, width), lambda i: (i, 0, 0)),
-            pl.BlockSpec((1, 8, width), lambda i: (i, 0, 0)),
-        ],
+        in_specs=[*of_block(states), pl.BlockSpec((1, 8, width), lambda i: (i, 0, 0))],
         out_specs=[
             whole((blocks, members + 8, members)),
             whole((members + 8, members)),
@@ -359,10 +357,12 @@
             jax.ShapeDtypeStruct((members + 8, members), F32),
         ],
         name="curvature",
-    )(states, obs)
-
-
-def transform_kernel(own, from_above, from_below, out, iterate, inverse):
+    )(*states, obs)
+
+
+def transform_kernel(edges, *refs):
+    own, *rest = refs
+    *halo, out, iterate, inverse = rest
     blocks, size, _ = iterate.shape
     row = lax.broadcasted_iota(jnp.int32, (size, size), 0)
     col = lax.broadcasted_iota(jnp.int32, (size, size), 1)
@@ -373,11 +373,10 @@
 
     norms, sides = [], []
     for b in range(blocks):
-        matrix, side = own[b, :size], own[b, size:]
-        if b == 0:
-            matrix, side = matrix + from_above[:size], side + from_above[size:]
-        if b == blocks - 1:
-            matrix, side = matrix + from_below[:size], side + from_below[size:]
+        place = b * (own.shape[0] - 1) if edges else b + 1
+        matrix, side = own[place, :size], own[place, size:]
+        if edges:
+            matrix, side = matrix + halo[b][:size], side + halo[b][size:]
         matrix = matrix + jnp.where(diagonal, size - 1.0, 0.0)
         squares = jnp.sum(jnp.sum(matrix * matrix, axis=0, keepdims=True), axis=1, keepdims=True)
         norm = jnp.sqrt(squares)
@@ -407,75 +406,96 @@
         out[b, size:] = shift
 
 
-def transforms(own, from_above, from_below):
-    blocks, _, size = own.shape
-    return pl.pallas_call(
-        transform_kernel,
-        out_shape=jax.ShapeDtypeStruct(own.shape, F32),
+def transforms(own, *halo):
+    total, lines, size = own.shape
+    blocks = len(halo) or total - 2
+    return pl.pallas_call(
+        partial(transform_kernel, bool(halo)),
+        out_shape=jax.ShapeDtypeStruct((blocks, lines, size), F32),
         scratch_shapes=[
             pltpu.VMEM((blocks, size, size), F32),
             pltpu.VMEM((blocks, size, size), F32),
         ],
         name="transform",
-    )(own, from_above, from_below)
-
-
-def apply_kernel(share, states, weights, out):
-    members = states.shape[1]
-    cells = states[0]
+    )(own, *halo)
+
+
+def apply_kernel(share, begin, pieces, *refs):
+    states, (inner, outer, out) = refs[:pieces], refs[pieces:]
+    block = pl.program_id(0)
+    within = (block > 0) & (block < pl.num_programs(0) - 1)
+    cells = jnp.concatenate([piece[0] for piece in states], 0)
+    members, width = cells.shape
+    rows = width // LANES
+    half = share // 2
+    weights = jnp.where(within, inner[0], outer[0])
     centre = jnp.sum(cells, axis=0, keepdims=True) * (1.0 / members)
-    moved = product(weights[0], cells - centre)
-    common_high, common_low = halves(centre + moved[members : members + 1])
-    common = jnp.concatenate(
-        [to_tile(common_high.astype(F32)), to_tile(common_low.astype(F32))], 0
-    ).astype(BF16)
+    moved = product(weights, cells - centre)
+    common = centre + moved[members : members + 1]
+    common_high, common_low = halves(
+        jnp.concatenate([common[:, r * LANES : (r + 1) * LANES] for r in range(rows)], 0)
+    )
     for part in range(members // share):
-        for r in range(ROWS):
-            out[0, part, r * share : (r + 1) * share] = moved[
-                part * share : (part + 1) * share, r * LANES : (r + 1) * LANES
-            ].astype(BF16)
-        out[0, part, ROWS * share :] = common
-
-
-def apply_transform(share, states, weights):
-    blocks, members, width = states.shape
-    lines = ROWS * share + 16
-    return pl.pallas_call(
-        partial(apply_kernel, share),
+        for r in range(rows):
+            for k in range(2):
+                at = k * (members // 2) + part * half
+                out[0, part, pl.ds(r * share + k * half, half)] = moved[
+                    at : at + half, r * LANES : (r + 1) * LANES
+                ].astype(BF16)
+        out[0, part, rows * share : rows * share + rows] = common_high
+        out[0, part, rows * share + rows :] = common_low
+
+
+def apply_transform(share, begin, rows, states, inner, outer):
+    blocks = states[0].shape[0]
+    members = sum(piece.shape[1] for piece in states)
+    lines = rows * (share + 2)
+    return pl.pallas_call(
+        partial(apply_kernel, share, begin, len(states)),
         grid=(blocks,),
         in_specs=[
-            pl.BlockSpec((1, members, width), lambda i: (i, 0, 0)),
-            pl.BlockSpec((1, members + 8, members), lambda i: (i, 0, 0)),
+            *[
+                pl.BlockSpec((1, piece.shape[1], rows * LANES), lambda i: (i, 0, begin))
+                for piece in states
+            ],
+            pl.BlockSpec(
+                (1, members + 8, members), lambda i: (jnp.clip(i - 1, 0, blocks - 3), 0, 0)
+            ),
+            pl.BlockSpec((1, members + 8, members), lambda i: (i // (blocks - 1), 0, 0)),
         ],
         out_specs=pl.BlockSpec((1, members // share, lines, LANES), lambda i: (i, 0, 0, 0)),
         out_shape=jax.ShapeDtypeStruct((blocks, members // share, lines, LANES), BF16),
         name="apply",
-    )(states, weights)
-
-
-def unpack_kernel(share, chunk, out, stage):
+    )(*states, inner, outer)
+
+
+def unpack_kernel(share, rows, *refs):
+    *chunks, out, stage = refs
     for part in range(PLANE):
         cols = slice(part * LANES, (part + 1) * LANES)
-        common = chunk[part, 0, ROWS * share :].astype(F32)
-        common = common[:ROWS] + common[ROWS:]
-        for r in range(ROWS):
-            field = chunk[part, 0, r * share : (r + 1) * share].astype(F32) + common[r : r + 1]
-            for k in range(share // 8):
-                stage[part, pl.ds(64 * k + r, 8, stride=8)] = field[8 * k : 8 * k + 8]
+        for half, chunk in enumerate(chunks):
+            common = chunk[part, 0, rows * share :].astype(F32)
+            common = common[:rows] + common[rows:]
+            for r in range(rows):
+                field = chunk[part, 0, r * share : (r + 1) * share].astype(F32) + common[r : r + 1]
+                for k in range(share // 8):
+                    stage[part, pl.ds(64 * k + half * rows + r, 8, stride=8)] = field[
+                        8 * k : 8 * k + 8
+                    ]
         out[:, cols] = stage[part]
 
 
-def unpack(share, chunk):
-    _, groups, lines, _ = chunk.shape
-    return pl.pallas_call(
-        partial(unpack_kernel, share),
+def unpack(share, rows, chunks):
+    _, groups, lines, _ = chunks[0].shape
+    return pl.pallas_call(
+        partial(unpack_kernel, share, rows),
         grid=(groups,),
-        in_specs=[pl.BlockSpec((PLANE, 1, lines, LANES), lambda i: (0, i, 0, 0))],
+        in_specs=[pl.BlockSpec((PLANE, 1, lines, LANES), lambda i: (0, i, 0, 0))] * len(chunks),
         out_specs=pl.BlockSpec((share * ROWS, PLANE * LANES), lambda i: (0, i)),
         out_shape=jax.ShapeDtypeStruct((share * ROWS, groups * PLANE * LANES), F32),
         scratch_shapes=[pltpu.VMEM((PLANE, share * ROWS, LANES), F32)],
         name="unpack",
-    )(chunk)
+    )(*chunks)
 
 
 def local(prior, drive, value, index, weight):
@@ -486,26 +506,43 @@
     upward = [(i + 1, i) for i in range(planes - 1)]
     downward = [(i, i + 1) for i in range(planes - 1)]
     me = lax.axis_index("member").reshape(1).astype(jnp.int32)
-    chunk, extra = pack(me, prior, drive, value, index, weight)
+    inside = jnp.stack([plane > 0, plane < planes - 1]).astype(F32)
+    axes = ("zc", "member")
+    tied = lax.optimization_barrier
+    extra = pack_extra(me, cols, drive, value, index, weight)
+    prior, extra = tied((prior, extra))
     extra = lax.all_to_all(extra, "zc", 0, 0, tiled=True)
-    chunk = lax.all_to_all(chunk, ("zc", "member"), 0, 0, tiled=True)
-    cells = chunk.reshape(PLANE, groups, ROWS + 1, members, LANES)
-    bottom = lax.ppermute(cells[0], "y", upward)
-    top = lax.ppermute(cells[PLANE - 1], "y", downward)
+    early, extra = tied((pack(prior, 0), extra))
+    early = lax.all_to_all(early, axes, 0, 0, tiled=True)
+    late = lax.all_to_all(pack(prior, 1), axes, 0, 0, tiled=True)
     drive_bottom = lax.ppermute(extra[0], "y", upward)
     drive_top = lax.ppermute(extra[PLANE - 1], "y", downward)
-    inside = jnp.stack([plane > 0, plane < planes - 1]).astype(F32)
-    states = forecast(inside, cells, top, bottom, extra, drive_top, drive_bottom)
+
+    def around(chunk):
+        cells = chunk.reshape(PLANE, groups, ROWS + 1, members // 2, LANES)
+        bottom = lax.ppermute(cells[0], "y", upward)
+        top = lax.ppermute(cells[PLANE - 1], "y", downward)
+        return inside, cells, top, bottom, extra, drive_top, drive_bottom
+
+    fields = around(early)
+    first = forecast(*fields, 0, groups // 2)
+    late, first = tied((late, first))
+    later = around(late)
+    second = forecast(*fields, groups // 2, groups)
+    third = forecast(*later, 0, groups)
+    states = (first, second, third)
     own, up, down = curvatures(states, extra)
     from_below = lax.ppermute(up, "y", upward)
     from_above = lax.ppermute(down, "y", downward)
-    weights = transforms(own, from_above, from_below)
-    analysed = apply_transform(members, states, weights)
-    lines = ROWS * members + 16
-    back = lax.all_to_all(
-        analysed.reshape(PLANE * groups, lines, LANES), ("zc", "member"), 0, 0, tiled=True
-    )
-    return unpack(members, back.reshape(PLANE, groups, lines, LANES)).reshape(members, rows, cols)
+    inner = transforms(own)
+    outer = transforms(own, from_above, from_below)
+    half = ROWS // 2
+    chunks = []
+    for begin in range(2):
+        analysed = apply_transform(members, begin, half, states, inner, outer)
+        sent = analysed.reshape(PLANE * groups, *analysed.shape[2:])
+        chunks.append(lax.all_to_all(sent, axes, 0, 0, tiled=True).reshape(analysed.shape))
+    return unpack(members, half, chunks).reshape(members, rows, cols)
 
 
 def solution(mesh):

time: 198 us -> 204 us (1.030)
  blocking collectives: 79.4 us -> 22.6 us
  starting transfers between devices: 20.2 us -> 47.8 us
  Pallas kernels: 83.9 us -> 101 us
  waiting for transfers between devices: 10.3 us -> 26.7 us
    all_to_all x2 -> x1, blocking collectives: 79.4 us -> 22.6 us  [local(): lax.all_to_all(sent, axes, 0, 0, tiled=True).reshape(analysed.shape)]
    all_to_all x0 -> x3, waiting for transfers between devices: none -> 26.1 us  [the longest x1 13.4 us: local(): lax.all_to_all(sent, axes, 0, 0, tiled=True).reshape(analysed.shape)]
    all_to_all x0 -> x3, starting transfers between devices: none -> 21.7 us  [the longest x1 9.54 us: local(): lax.all_to_all(sent, axes, 0, 0, tiled=True).reshape(analysed.shape)]
    pallas_call x6 -> x12, Pallas kernels: 83.9 us -> 101 us  [the longest x3 46.9 us: forecast(): pl.pallas_call(forecast_kernel, grid=((end - begin) // 2,), in_specs=[pl....]
    ppermute x2 -> x4, starting transfers between devices: 6.11 us -> 11.3 us  [the longest x2 8.76 us: around(): top = lax.ppermute(cells[PLANE - 1], 'y', downward)]
    all_to_all x1, waiting for transfers between devices: 3.86 us -> 0.01 us  [local(): extra = lax.all_to_all(extra, 'zc', 0, 0, tiled=True)]
    ppermute x1, waiting for transfers between devices: 3.46 us -> 0.01 us  [local(): from_below = lax.ppermute(up, 'y', upward)]
    ppermute x1, waiting for transfers between devices: 2.65 us -> 0.01 us  [local(): from_above = lax.ppermute(down, 'y', downward)]
  transfers between devices with their start and end apart: 7 -> 12, of which waited for: 4 -> 3; matrix products, arithmetic and copies ran while one was open for 0% -> 0% of each run, Pallas kernels for 0% -> 25%
where the time goes in v1:
time: 204 us; the launch traced here: 202 us
  Pallas kernels  101 us (50%)
  starting transfers between devices  47.8 us (23%)
  waiting for transfers between devices  26.7 us (13%)
  blocking collectives  22.6 us (11%)
  local copies, waits for them, and re-layouts  3.1 us (2%)
    pallas_call x3, Pallas kernels, forecast(): pl.pallas_call(forecast_kernel, grid=((end - begin) // 2,), in_specs=[pl....  46.9 us
    all_to_all x1, blocking collectives, local(): lax.all_to_all(sent, axes, 0, 0, tiled=True).reshape(analysed.shape)  22.6 us
    pallas_call x2, Pallas kernels, transforms(): pl.pallas_call(partial(transform_kernel, bool(halo)), out_shape=jax.Shape...  15.6 us
    all_to_all x1, waiting for transfers between devices, local(): lax.all_to_all(sent, axes, 0, 0, tiled=True).reshape(analysed.shape)  13.4 us
    all_to_all x1, waiting for transfers between devices, local(): early = lax.all_to_all(early, axes, 0, 0, tiled=True)  12.7 us
    pallas_call x2, Pallas kernels, pack(): pl.pallas_call(partial(pack_kernel, tiles), grid=(1,), in_specs=[pl.Block...  12.6 us
    pallas_call x2, Pallas kernels, apply_transform(): pl.pallas_call(partial(apply_kernel, share, begin, len(states)), grid=(bl...  9.66 us
    all_to_all x1, starting transfers between devices, local(): lax.all_to_all(sent, axes, 0, 0, tiled=True).reshape(analysed.shape)  9.54 us
  transfers between devices with their start and end apart: 12, of which 3 were waited for; matrix products, arithmetic and copies ran while one was open for 0% of the time, Pallas kernels for 25%

profile of v1, /device:TPU:1, one launch (start us, length us, event | category | flops | bytes accessed | tf_op | source)
XLA Modules:
  0.0 202.0 jit_solution(3950820173388378983)
XLA Ops:
  0.0 1.8 pack_extra.1
  1.8 4.7 %all-to-all-start.1 = ((f32[4,8,1024]{2,1,0:T(8,128)}), f32[4,8,1024]{2,1,0:T(8,128)S(1)}, u32[]{:S(2)}, u32[]{:S(2)}) async-start(f32[4,8,1024]{2,1,0:T(8,128)} %pack_extra.1), calls=%async_computation.1 | async-start | bytes 262144 | tf_op jit(solution)/shard_map/all_to_all | solution.py:514
  6.5 6.3 %pack.3 = bf16[32,9,16,128]{3,2,1,0:T(8,128)(2,1)} custom-call(f32[256,4096]{1,0:T(8,128)} %bitcast.15), custom_call_target="tpu_custom_call" | custom-call | tf_op jit(solution)/shard_map/pack/pallas_call | solution.py:131
  12.8 0.0 all-to-all-done.1.drive.refs_3_
  12.8 0.0 copy-start.3
  12.8 8.4 %all-to-all-start.2 = ((bf16[32,9,16,128]{3,2,1,0:T(8,128)(2,1)}), bf16[32,9,16,128]{3,2,1,0:T(8,128)(2,1)S(1)}, u32[]{:S(2)}, u32[]{:S(2)}) async-start(bf16[32,9,16,128]{3,2,1,0:T(8,128)(2,1)} %pack.3), calls=%async_computation.2 | async-start | bytes 2359296 | tf_op jit(solution)/shard_map/all_to_all | solution.py:516
  21.2 6.3 %pack.2 = bf16[32,9,16,128]{3,2,1,0:T(8,128)(2,1)} custom-call(f32[256,4096]{1,0:T(8,128)} %bitcast.16), custom_call_target="tpu_custom_call" | custom-call | tf_op jit(solution)/shard_map/pack/pallas_call | solution.py:131
  27.5 12.7 %all-to-all-done.2 = bf16[32,9,16,128]{3,2,1,0:T(8,128)(2,1)S(1)} async-done(((bf16[32,9,16,128]{3,2,1,0:T(8,128)(2,1)}), bf16[32,9,16,128]{3,2,1,0:T(8,128)(2,1)S(1)}, u32[]{:S(2)}, u32[]{:S(2)}) %all-to-all-start.2) | async-done | bytes 1179680 | tf_op jit(solution)/shard_map/all_to_all | solution.py:516
  40.2 0.0 copy-start
  40.2 3.7 %all-to-all-start = ((bf16[32,9,16,128]{3,2,1,0:T(8,128)(2,1)}), bf16[32,9,16,128]{3,2,1,0:T(8,128)(2,1)S(1)}, u32[]{:S(2)}, u32[]{:S(2)}) async-start(bf16[32,9,16,128]{3,2,1,0:T(8,128)(2,1)} %pack.2), calls=%async_computation | async-start | bytes 2359296 | tf_op jit(solution)/shard_map/all_to_all | solution.py:517
  44.0 0.0 copy-done
  44.0 1.3 collective-permute-start.1
  45.4 4.0 %collective-permute-start = (bf16[8,9,16,128]{3,2,1,0:T(8,128)(2,1)S(1)}, bf16[8,9,16,128]{3,2,1,0:T(8,128)(2,1)S(1)}, u32[]{:S(2)}, u32[]{:S(2)}) collective-permute-start(bf16[8,9,16,128]{3,2,1,0:T(8,128)(2,1)S(1)} %get-tuple-element.26), channel_id=1, source_target_pairs={{0,4},{4,8},{8,12},{1,5},{5,9},{9,13},{2,6},{6,10},{10,14},{3,7},{... | collective-permute-start | bytes 884744 | tf_op jit(solution)/shard_map/ppermute | solution.py:524
  49.4 0.0 copy-done.3
  49.4 1.3 collective-permute-start.3
  50.7 4.0 %collective-permute-start.2 = (f32[8,1024]{1,0:T(8,128)S(1)}, f32[8,1024]{1,0:T(8,128)S(1)}, u32[]{:S(2)}, u32[]{:S(2)}) collective-permute-start(f32[8,1024]{1,0:T(8,128)S(1)} %get-tuple-element.28), channel_id=1, source_target_pairs={{0,4},{4,8},{8,12},{1,5},{5,9},{9,13},{2,6},{6,10},{10,14},{3,7},{... | collective-permute-start | bytes 98312 | tf_op jit(solution)/shard_map/ppermute | solution.py:519
  54.7 0.6 add_convert_fusion.inside
  55.3 0.0 collective-permute-done.3.drive_bottom
  55.3 0.0 copy-start.6
  55.3 0.6 collective-permute-done.2.drive_top
  55.9 0.0 copy-start.7
  55.9 0.0 collective-permute-done.1.bottom
  55.9 0.0 copy-start.4
  55.9 0.0 collective-permute-done.top
  55.9 0.0 copy-start.5
  55.9 0.0 copy-done.6
  55.9 0.6 copy-done.7
  56.5 0.1 copy-done.4
  56.6 0.1 copy-done.5
  56.7 12.2 %forecast.3.refs_0_ = f32[4,64,1024]{2,1,0:T(8,128)} custom-call(f32[2]{0:T(128)} %add_convert_fusion.inside, bf16[4,8,9,16,128]{4,3,2,1,0:T(8,128)(2,1)} %bitcast.17, bf16[8,9,16,128]{3,2,1,0:T(8,128)(2,1)} %copy-done.5, bf16[8,9,16,128]{3,2,1,0:T(8,128)(2,1)} %copy-done.4, f32[4,8,1024]{2,1,0:T(8,128)} %copy-done.3, f32[8,1024]{1,0:T(8,128)} %copy-done.7, ...), custom_call_target="tpu_custom_call" | custom-call | tf_op jit(solution)/shard_map/forecast/pallas_call | solution.py:228
  68.9 0.0 all-to-all-done
  68.9 0.0 copy-start.1
  69.0 1.3 collective-permute-start.5
  70.3 4.8 %collective-permute-start.4 = (bf16[8,9,16,128]{3,2,1,0:T(8,128)(2,1)S(1)}, bf16[8,9,16,128]{3,2,1,0:T(8,128)(2,1)S(1)}, u32[]{:S(2)}, u32[]{:S(2)}) collective-permute-start(bf16[8,9,16,128]{3,2,1,0:T(8,128)(2,1)S(1)} %get-tuple-element.24), channel_id=1, source_target_pairs={{0,4},{4,8},{8,12},{1,5},{5,9},{9,13},{2,6},{6,10},{10,14},{3,7},{... | collective-permute-start | bytes 884744 | tf_op jit(solution)/shard_map/ppermute | solution.py:524
  75.0 12.2 %forecast.4.refs_1_ = f32[4,64,1024]{2,1,0:T(8,128)} custom-call(f32[2]{0:T(128)} %add_convert_fusion.inside, bf16[4,8,9,16,128]{4,3,2,1,0:T(8,128)(2,1)} %bitcast.18, bf16[8,9,16,128]{3,2,1,0:T(8,128)(2,1)} %copy-done.5, bf16[8,9,16,128]{3,2,1,0:T(8,128)(2,1)} %copy-done.4, f32[4,8,1024]{2,1,0:T(8,128)} %copy-done.3, f32[8,1024]{1,0:T(8,128)} %copy-done.7, ...), custom_call_target="tpu_custom_call" | custom-call | tf_op jit(solution)/shard_map/forecast/pallas_call | solution.py:228
  87.3 0.0 copy-done.1
  87.3 0.0 collective-permute-done.5.bottom
  87.3 0.0 copy-start.8
  87.3 0.0 collective-permute-done.4.top
  87.3 0.0 copy-start.9
  87.3 0.7 copy-done.8
  88.0 0.1 copy-done.9
  88.1 22.5 %forecast.5.refs_2_ = f32[4,128,1024]{2,1,0:T(8,128)} custom-call(f32[2]{0:T(128)} %add_convert_fusion.inside, bf16[4,8,9,16,128]{4,3,2,1,0:T(8,128)(2,1)} %bitcast.19, bf16[8,9,16,128]{3,2,1,0:T(8,128)(2,1)} %copy-done.9, bf16[8,9,16,128]{3,2,1,0:T(8,128)(2,1)} %copy-done.8, f32[4,8,1024]{2,1,0:T(8,128)} %copy-done.3, f32[8,1024]{1,0:T(8,128)} %copy-done.7, ...), custom_call_target="tpu_custom_call" | custom-call | tf_op jit(solution)/shard_map/forecast/pallas_call | solution.py:228
  110.6 7.6 %curvature.1 = (f32[4,264,256]{2,1,0:T(8,128)}, f32[264,256]{1,0:T(8,128)}, f32[264,256]{1,0:T(8,128)}) custom-call(f32[4,64,1024]{2,1,0:T(8,128)} %forecast.3.refs_0_, f32[4,64,1024]{2,1,0:T(8,128)} %forecast.4.refs_1_, f32[4,128,1024]{2,1,0:T(8,128)} %forecast.5.refs_2_, f32[4,8,1024]{2,1,0:T(8,128)} %copy-done.3), custom_call_target="tpu_custom_call" | custom-call | tf_op jit(solution)/shard_map/curvature/pallas_call | solution.py:345
  118.1 3.3 %collective-permute-start.6 = (f32[264,256]{1,0:T(8,128)}, f32[264,256]{1,0:T(8,128)S(1)}, u32[]{:S(2)}, u32[]{:S(2)}) collective-permute-start(f32[264,256]{1,0:T(8,128)} %get-tuple-element.21), channel_id=1, source_target_pairs={{0,4},{4,8},{8,12},{1,5},{5,9},{9,13},{2,6},{6,10},{10,14},{3,7},{... | collective-permute-start | bytes 811016 | tf_op jit(solution)/shard_map/ppermute | solution.py:536
  121.5 1.5 collective-permute-start.7
  123.0 7.7 %transform.2.refs_3_ = f32[2,264,256]{2,1,0:T(8,128)} custom-call(f32[4,264,256]{2,1,0:T(8,128)} %get-tuple-element.20.refs_0_), custom_call_target="tpu_custom_call" | custom-call | tf_op jit(solution)/shard_map/transform/pallas_call | solution.py:412
  130.7 0.0 collective-permute-done.6.refs_1_
  130.7 0.0 copy-start.10
  130.7 0.0 collective-permute-done.7.refs_2_
  130.7 0.7 copy-done.10
  131.4 0.0 copy-start.11
  131.4 0.7 copy-done.11
  132.1 7.9 %transform.3.refs_4_ = f32[2,264,256]{2,1,0:T(8,128)} custom-call(f32[4,264,256]{2,1,0:T(8,128)} %get-tuple-element.20.refs_0_, f32[264,256]{1,0:T(8,128)} %copy-done.10, f32[264,256]{1,0:T(8,128)} %copy-done.11), custom_call_target="tpu_custom_call" | custom-call | tf_op jit(solution)/shard_map/transform/pallas_call | solution.py:412
  140.0 4.8 %apply.3 = bf16[4,8,136,128]{3,2,1,0:T(8,128)(2,1)} custom-call(f32[4,64,1024]{2,1,0:T(8,128)} %forecast.3.refs_0_, f32[4,64,1024]{2,1,0:T(8,128)} %forecast.4.refs_1_, f32[4,128,1024]{2,1,0:T(8,128)} %forecast.5.refs_2_, f32[2,264,256]{2,1,0:T(8,128)} %transform.2.refs_3_, f32[2,264,256]{2,1,0:T(8,128)} %transform.3.refs_4_), custom_call_target="tpu_custom_call" | custom-call | tf_op jit(solution)/shard_map/apply/pallas_call | solution.py:453
  144.8 9.5 %all-to-all-start.4 = ((bf16[32,136,128]{2,1,0:T(8,128)(2,1)}), bf16[32,136,128]{2,1,0:T(8,128)(2,1)S(1)}, u32[]{:S(2)}, u32[]{:S(2)}) async-start(bf16[32,136,128]{2,1,0:T(8,128)(2,1)} %bitcast.22), calls=%async_computation.4 | async-start | bytes 2228224 | tf_op jit(solution)/shard_map/all_to_all | solution.py:544
  154.4 4.8 %apply.2 = bf16[4,8,136,128]{3,2,1,0:T(8,128)(2,1)} custom-call(f32[4,64,1024]{2,1,0:T(8,128)} %forecast.3.refs_0_, f32[4,64,1024]{2,1,0:T(8,128)} %forecast.4.refs_1_, f32[4,128,1024]{2,1,0:T(8,128)} %forecast.5.refs_2_, f32[2,264,256]{2,1,0:T(8,128)} %transform.2.refs_3_, f32[2,264,256]{2,1,0:T(8,128)} %transform.3.refs_4_), custom_call_target="tpu_custom_call" | custom-call | tf_op jit(solution)/shard_map/apply/pallas_call | solution.py:453
  159.2 13.4 %all-to-all-done.4 = bf16[32,136,128]{2,1,0:T(8,128)(2,1)S(1)} async-done(((bf16[32,136,128]{2,1,0:T(8,128)(2,1)}), bf16[32,136,128]{2,1,0:T(8,128)(2,1)S(1)}, u32[]{:S(2)}, u32[]{:S(2)}) %all-to-all-start.4) | async-done | bytes 1114144 | tf_op jit(solution)/shard_map/all_to_all | solution.py:544
  172.6 0.0 copy-start.2
  172.6 22.6 %all_to_all.25 = bf16[32,136,128]{2,1,0:T(8,128)(2,1)} all-to-all(bf16[32,136,128]{2,1,0:T(8,128)(2,1)} %bitcast.23), channel_id=1, replica_groups=mesh['member'=8,'y'=4,'zc'=4] {'zc','member'}, dimensions={0} | all-to-all | bytes 2228224 | tf_op jit(solution)/shard_map/all_to_all | solution.py:544
  195.3 0.0 copy-done.2
  195.3 6.8 %unpack.1 = f32[256,4096]{1,0:T(8,128)} custom-call(bf16[4,8,136,128]{3,2,1,0:T(8,128)(2,1)} %bitcast.21, bf16[4,8,136,128]{3,2,1,0:T(8,128)(2,1)} %bitcast.20), custom_call_target="tpu_custom_call" | custom-call | tf_op jit(solution)/shard_map/unpack/pallas_call | solution.py:490
  (3 shorter events, 0.1 us)
Async XLA Ops:
  1.8 11.0 %all-to-all-start.1 = ((f32[4,8,1024]{2,1,0:T(8,128)}), f32[4,8,1024]{2,1,0:T(8,128)S(1)}, u32[]{:S(2)}, u32[]{:S(2)}) async-start(f32[4,8,1024]{2,1,0:T(8,128)} %pack_extra.1), calls=%async_computation.1 | async-start | bytes 262144 | tf_op jit(solution)/shard_map/all_to_all | solution.py:514
  12.8 36.6 %copy-start.3 = (f32[4,8,1024]{2,1,0:T(8,128)}, f32[4,8,1024]{2,1,0:T(8,128)S(1)}, u32[]{:S(2)}) copy-start(f32[4,8,1024]{2,1,0:T(8,128)S(1)} %all-to-all-done.1.drive.refs_3_) | copy-start | bytes 393220
  12.8 27.4 %all-to-all-start.2 = ((bf16[32,9,16,128]{3,2,1,0:T(8,128)(2,1)}), bf16[32,9,16,128]{3,2,1,0:T(8,128)(2,1)S(1)}, u32[]{:S(2)}, u32[]{:S(2)}) async-start(bf16[32,9,16,128]{3,2,1,0:T(8,128)(2,1)} %pack.3), calls=%async_computation.2 | async-start | bytes 2359296 | tf_op jit(solution)/shard_map/all_to_all | solution.py:516
  40.2 3.8 %copy-start = (bf16[32,9,16,128]{3,2,1,0:T(8,128)(2,1)}, bf16[32,9,16,128]{3,2,1,0:T(8,128)(2,1)S(1)}, u32[]{:S(2)}) copy-start(bf16[32,9,16,128]{3,2,1,0:T(8,128)(2,1)S(1)} %all-to-all-done.2) | copy-start | bytes 3538948
  40.2 28.7 %all-to-all-start = ((bf16[32,9,16,128]{3,2,1,0:T(8,128)(2,1)}), bf16[32,9,16,128]{3,2,1,0:T(8,128)(2,1)S(1)}, u32[]{:S(2)}, u32[]{:S(2)}) async-start(bf16[32,9,16,128]{3,2,1,0:T(8,128)(2,1)} %pack.2), calls=%async_computation | async-start | bytes 2359296 | tf_op jit(solution)/shard_map/all_to_all | solution.py:517
  44.0 11.8 %collective-permute-start.1 = (bf16[8,9,16,128]{3,2,1,0:T(8,128)(2,1)S(1)}, bf16[8,9,16,128]{3,2,1,0:T(8,128)(2,1)S(1)}, u32[]{:S(2)}, u32[]{:S(2)}) collective-permute-start(bf16[8,9,16,128]{3,2,1,0:T(8,128)(2,1)S(1)} %get-tuple-element.25), channel_id=1, source_target_pairs={{4,0},{8,4},{12,8},{5,1},{9,5},{13,9},{6,2},{10,6},{14,10},{7,3},{... | collective-permute-start | bytes 884744 | tf_op jit(solution)/shard_map/ppermute | solution.py:523
  45.4 10.5 %collective-permute-start = (bf16[8,9,16,128]{3,2,1,0:T(8,128)(2,1)S(1)}, bf16[8,9,16,128]{3,2,1,0:T(8,128)(2,1)S(1)}, u32[]{:S(2)}, u32[]{:S(2)}) collective-permute-start(bf16[8,9,16,128]{3,2,1,0:T(8,128)(2,1)S(1)} %get-tuple-element.26), channel_id=1, source_target_pairs={{0,4},{4,8},{8,12},{1,5},{5,9},{9,13},{2,6},{6,10},{10,14},{3,7},{... | collective-permute-start | bytes 884744 | tf_op jit(solution)/shard_map/ppermute | solution.py:524
  49.4 5.9 %collective-permute-start.3 = (f32[8,1024]{1,0:T(8,128)S(1)}, f32[8,1024]{1,0:T(8,128)S(1)}, u32[]{:S(2)}, u32[]{:S(2)}) collective-permute-start(f32[8,1024]{1,0:T(8,128)S(1)} %get-tuple-element.27), channel_id=1, source_target_pairs={{4,0},{8,4},{12,8},{5,1},{9,5},{13,9},{6,2},{10,6},{14,10},{7,3},{... | collective-permute-start | bytes 98312 | tf_op jit(solution)/shard_map/ppermute | solution.py:518
  50.7 5.2 %collective-permute-start.2 = (f32[8,1024]{1,0:T(8,128)S(1)}, f32[8,1024]{1,0:T(8,128)S(1)}, u32[]{:S(2)}, u32[]{:S(2)}) collective-permute-start(f32[8,1024]{1,0:T(8,128)S(1)} %get-tuple-element.28), channel_id=1, source_target_pairs={{0,4},{4,8},{8,12},{1,5},{5,9},{9,13},{2,6},{6,10},{10,14},{3,7},{... | collective-permute-start | bytes 98312 | tf_op jit(solution)/shard_map/ppermute | solution.py:519
  55.3 0.6 copy-start.6
  55.9 0.6 copy-start.7
  55.9 0.7 copy-start.4
  55.9 0.8 copy-start.5
  68.9 18.4 %copy-start.1 = (bf16[32,9,16,128]{3,2,1,0:T(8,128)(2,1)}, bf16[32,9,16,128]{3,2,1,0:T(8,128)(2,1)S(1)}, u32[]{:S(2)}) copy-start(bf16[32,9,16,128]{3,2,1,0:T(8,128)(2,1)S(1)} %all-to-all-done) | copy-start | bytes 3538948
  69.0 18.3 %collective-permute-start.5 = (bf16[8,9,16,128]{3,2,1,0:T(8,128)(2,1)S(1)}, bf16[8,9,16,128]{3,2,1,0:T(8,128)(2,1)S(1)}, u32[]{:S(2)}, u32[]{:S(2)}) collective-permute-start(bf16[8,9,16,128]{3,2,1,0:T(8,128)(2,1)S(1)} %get-tuple-element.23), channel_id=1, source_target_pairs={{4,0},{8,4},{12,8},{5,1},{9,5},{13,9},{6,2},{10,6},{14,10},{7,3},{... | collective-permute-start | bytes 884744 | tf_op jit(solution)/shard_map/ppermute | solution.py:523
  70.3 17.0 %collective-permute-start.4 = (bf16[8,9,16,128]{3,2,1,0:T(8,128)(2,1)S(1)}, bf16[8,9,16,128]{3,2,1,0:T(8,128)(2,1)S(1)}, u32[]{:S(2)}, u32[]{:S(2)}) collective-permute-start(bf16[8,9,16,128]{3,2,1,0:T(8,128)(2,1)S(1)} %get-tuple-element.24), channel_id=1, source_target_pairs={{0,4},{4,8},{8,12},{1,5},{5,9},{9,13},{2,6},{6,10},{10,14},{3,7},{... | collective-permute-start | bytes 884744 | tf_op jit(solution)/shard_map/ppermute | solution.py:524
  87.3 0.7 copy-start.8
  87.3 0.8 copy-start.9
  118.1 12.6 %collective-permute-start.6 = (f32[264,256]{1,0:T(8,128)}, f32[264,256]{1,0:T(8,128)S(1)}, u32[]{:S(2)}, u32[]{:S(2)}) collective-permute-start(f32[264,256]{1,0:T(8,128)} %get-tuple-element.21), channel_id=1, source_target_pairs={{0,4},{4,8},{8,12},{1,5},{5,9},{9,13},{2,6},{6,10},{10,14},{3,7},{... | collective-permute-start | bytes 811016 | tf_op jit(solution)/shard_map/ppermute | solution.py:536
  121.5 9.2 %collective-permute-start.7 = (f32[264,256]{1,0:T(8,128)}, f32[264,256]{1,0:T(8,128)S(1)}, u32[]{:S(2)}, u32[]{:S(2)}) collective-permute-start(f32[264,256]{1,0:T(8,128)} %get-tuple-element.22), channel_id=1, source_target_pairs={{4,0},{8,4},{12,8},{5,1},{9,5},{13,9},{6,2},{10,6},{14,10},{7,3},{... | collective-permute-start | bytes 811016 | tf_op jit(solution)/shard_map/ppermute | solution.py:535
  130.7 0.7 copy-start.10
  131.4 0.7 copy-start.11
  144.8 27.8 %all-to-all-start.4 = ((bf16[32,136,128]{2,1,0:T(8,128)(2,1)}), bf16[32,136,128]{2,1,0:T(8,128)(2,1)S(1)}, u32[]{:S(2)}, u32[]{:S(2)}) async-start(bf16[32,136,128]{2,1,0:T(8,128)(2,1)} %bitcast.22), calls=%async_computation.4 | async-start | bytes 2228224 | tf_op jit(solution)/shard_map/all_to_all | solution.py:544
  172.6 22.6 %copy-start.2 = (bf16[32,136,128]{2,1,0:T(8,128)(2,1)}, bf16[32,136,128]{2,1,0:T(8,128)(2,1)S(1)}, u32[]{:S(2)}) copy-start(bf16[32,136,128]{2,1,0:T(8,128)(2,1)S(1)} %all-to-all-done.4) | copy-start | bytes 3342340

commit v2 on v1

--- a/solution.py
+++ b/solution.py
@@ -7,6 +7,7 @@
 from jax.experimental import pallas as pl
 from jax.experimental.pallas import tpu as pltpu
 from jax.sharding import Mesh, PartitionSpec as P
+
 
 STEPS = 8
 ITERS = 6
@@ -90,7 +91,9 @@
 def extra_kernel(tiles, me_ref, drive, value, index, weight, extra):
     lane8 = lane_index(8)
     weights = weight[0].astype(F32)
-    for part in range(PLANE):
+    slot4 = lax.broadcasted_iota(jnp.int32, weights.shape, 0)
+    for ahead in range(PLANE):
+        part = lax.rem(me_ref[1] + ahead, PLANE)
         tile = me_ref[0] * PLANE + part
 
         def forcing(t):
@@ -105,13 +108,14 @@
         low = low + pltpu.roll(low, 64, 1)
         high = high + pltpu.roll(high, 32, 1)
         high = high + pltpu.roll(high, 64, 1)
-        extra[part, 0:1, :] = value[0, part : part + 1, :]
-        extra[part, 1:2, :] = index[0, part : part + 1, :].astype(F32)
-        extra[part, 2:3, :] = weights[part : part + 1, :]
+        chosen = slot4 == part
+        for slot, field in ((0, value[0]), (1, index[0].astype(F32)), (2, weights)):
+            line = jnp.sum(jnp.where(chosen, field, 0.0), axis=0, keepdims=True)
+            extra[ahead, slot : slot + 1, :] = line
         for slot, field in ((3, main), (4, low), (5, high)):
             for row in range(ROWS):
-                extra[part, slot : slot + 1, row * LANES : (row + 1) * LANES] = field[row : row + 1]
-        extra[part, 6:8, :] = jnp.zeros((2, ROWS * LANES), F32)
+                extra[ahead, slot : slot + 1, row * LANES : (row + 1) * LANES] = field[row : row + 1]
+        extra[ahead, 6:8, :] = jnp.zeros((2, ROWS * LANES), F32)
 
 
 def pack_extra(me, cols, drive, value, index, weight):
@@ -139,24 +143,42 @@
     )(prior.reshape(members * rows, cols))
 
 
-def forecast_kernel(inside, cells, top, bottom, drive, drive_top, drive_bottom, out, state, force):
+def force_kernel(me_ref, own, one, two, three, extra, force, halo):
+    for behind, came in enumerate((own, one, two, three)):
+        strip = lax.rem(me_ref[1] + PLANE - behind, PLANE)
+        extra[strip] = came[:8]
+        halo[strip] = came[8:]
+    for row in range((PLANE + 2) * ROWS):
+        strip, r = divmod(row, ROWS)
+        if strip == 0:
+            source = halo.at[PLANE - 1]
+        elif strip == PLANE + 1:
+            source = halo.at[0]
+        else:
+            source = extra.at[strip - 1]
+        for slot in range(3):
+            line = source[3 + slot : 4 + slot, r * LANES : (r + 1) * LANES]
+            force[slot, row] = jnp.broadcast_to(line * 0.005, (8, LANES))
+
+
+def forcing(me, pieces):
+    width = pieces[0].shape[1]
+    return pl.pallas_call(
+        force_kernel,
+        in_specs=[pl.BlockSpec(memory_space=pltpu.SMEM)]
+        + [pl.BlockSpec(memory_space=pltpu.VMEM)] * PLANE,
+        out_shape=[
+            jax.ShapeDtypeStruct((PLANE, 8, width), F32),
+            jax.ShapeDtypeStruct((3, (PLANE + 2) * ROWS, 8, LANES), F32),
+        ],
+        scratch_shapes=[pltpu.VMEM((PLANE, 8, width), F32)],
+        name="forcing",
+    )(me, *pieces)
+
+
+def forecast_kernel(inside, cells, top, bottom, force, out, state):
     depth = (PLANE + 2) * ROWS
     lane = lane_index(8)
-
-    @pl.when(pl.program_id(0) == 0)
-    def _():
-        for row in range(depth):
-            strip, r = divmod(row, ROWS)
-            spot = slice(r * LANES, (r + 1) * LANES)
-            for slot in range(3):
-                pick = slice(3 + slot, 4 + slot)
-                if strip == 0:
-                    line = drive_top[pick, spot]
-                elif strip == PLANE + 1:
-                    line = drive_bottom[pick, spot]
-                else:
-                    line = drive[strip - 1, pick, spot]
-                force[slot, row] = jnp.broadcast_to(line * 0.005, (8, LANES))
 
     for row in range(depth):
         strip, r = divmod(row, ROWS)
@@ -221,7 +243,7 @@
             )
 
 
-def forecast(inside, cells, top, bottom, drive, drive_top, drive_bottom, begin, end):
+def forecast(inside, cells, top, bottom, force, begin, end):
     _, _, lines, members, _ = cells.shape
     at = begin // 2
     whole = lambda shape: pl.BlockSpec(shape, lambda i: (0,) * len(shape))
@@ -233,18 +255,15 @@
             pl.BlockSpec((PLANE, 2, lines, members, LANES), lambda i: (0, i + at, 0, 0, 0)),
             pl.BlockSpec((2, lines, members, LANES), lambda i: (i + at, 0, 0, 0)),
             pl.BlockSpec((2, lines, members, LANES), lambda i: (i + at, 0, 0, 0)),
-            whole(drive.shape),
-            whole(drive_top.shape),
-            whole(drive_bottom.shape),
+            whole(force.shape),
         ],
         out_specs=pl.BlockSpec((PLANE, 2 * members, ROWS * LANES), lambda i: (0, i, 0)),
         out_shape=jax.ShapeDtypeStruct((PLANE, (end - begin) * members, ROWS * LANES), F32),
         scratch_shapes=[
             pltpu.VMEM((6, (PLANE + 2) * ROWS, 8, LANES), F32),
-            pltpu.VMEM((3, (PLANE + 2) * ROWS, 8, LANES), F32),
         ],
         name="forecast",
-    )(inside, cells, top, bottom, drive, drive_top, drive_bottom)
+    )(inside, cells, top, bottom, force)
 
 
 def to_tile(line):
@@ -420,7 +439,7 @@
     )(own, *halo)
 
 
-def apply_kernel(share, begin, pieces, *refs):
+def apply_kernel(share, pieces, *refs):
     states, (inner, outer, out) = refs[:pieces], refs[pieces:]
     block = pl.program_id(0)
     within = (block > 0) & (block < pl.num_programs(0) - 1)
@@ -451,7 +470,7 @@
     members = sum(piece.shape[1] for piece in states)
     lines = rows * (share + 2)
     return pl.pallas_call(
-        partial(apply_kernel, share, begin, len(states)),
+        partial(apply_kernel, share, len(states)),
         grid=(blocks,),
         in_specs=[
             *[
@@ -505,24 +524,33 @@
     plane = lax.axis_index("y")
     upward = [(i + 1, i) for i in range(planes - 1)]
     downward = [(i, i + 1) for i in range(planes - 1)]
-    me = lax.axis_index("member").reshape(1).astype(jnp.int32)
+    me = jnp.stack([lax.axis_index("member"), lax.axis_index("zc")]).astype(jnp.int32)
     inside = jnp.stack([plane > 0, plane < planes - 1]).astype(F32)
     axes = ("zc", "member")
     tied = lax.optimization_barrier
+    early, drive = tied((pack(prior, 0), drive))
+    outward = [
+        (PLANE * i + edge, PLANE * j + edge)
+        for edge, pairs in ((0, upward), (PLANE - 1, downward))
+        for i, j in pairs
+    ]
     extra = pack_extra(me, cols, drive, value, index, weight)
-    prior, extra = tied((prior, extra))
-    extra = lax.all_to_all(extra, "zc", 0, 0, tiled=True)
-    early, extra = tied((pack(prior, 0), extra))
+    outer_rows = lax.ppermute(extra, ("y", "zc"), outward)
+    pieces = [jnp.concatenate([extra[d], outer_rows[d]], 0) for d in range(PLANE)]
+    for d in range(1, PLANE):
+        pieces[d] = lax.ppermute(
+            pieces[d], "zc", [(i, (i + d) % PLANE) for i in range(PLANE)]
+        )
+    extra, force = forcing(me, pieces)
     early = lax.all_to_all(early, axes, 0, 0, tiled=True)
-    late = lax.all_to_all(pack(prior, 1), axes, 0, 0, tiled=True)
-    drive_bottom = lax.ppermute(extra[0], "y", upward)
-    drive_top = lax.ppermute(extra[PLANE - 1], "y", downward)
+    late = pack(prior, 1)
+    late = lax.all_to_all(late, axes, 0, 0, tiled=True)
 
     def around(chunk):
         cells = chunk.reshape(PLANE, groups, ROWS + 1, members // 2, LANES)
         bottom = lax.ppermute(cells[0], "y", upward)
         top = lax.ppermute(cells[PLANE - 1], "y", downward)
-        return inside, cells, top, bottom, extra, drive_top, drive_bottom
+        return inside, cells, top, bottom, force
 
     fields = around(early)
     first = forecast(*fields, 0, groups // 2)
@@ -536,13 +564,10 @@
     from_above = lax.ppermute(down, "y", downward)
     inner = transforms(own)
     outer = transforms(own, from_above, from_below)
-    half = ROWS // 2
-    chunks = []
-    for begin in range(2):
-        analysed = apply_transform(members, begin, half, states, inner, outer)
-        sent = analysed.reshape(PLANE * groups, *analysed.shape[2:])
-        chunks.append(lax.all_to_all(sent, axes, 0, 0, tiled=True).reshape(analysed.shape))
-    return unpack(members, half, chunks).reshape(members, rows, cols)
+    analysed = apply_transform(members, 0, ROWS, states, inner, outer)
+    sent = analysed.reshape(PLANE * groups, *analysed.shape[2:])
+    back = lax.all_to_all(sent, axes, 0, 0, tiled=True).reshape(analysed.shape)
+    return unpack(members, ROWS, [back]).reshape(members, rows, cols)
 
 
 def solution(mesh):

time: 204 us -> 195 us (0.956)
  blocking collectives: 22.6 us -> 38.5 us
  starting transfers between devices: 47.8 us -> 32 us
  waiting for transfers between devices: 26.7 us -> 18.2 us
    all_to_all x1, blocking collectives: 22.6 us -> 38.5 us  [local(): back = lax.all_to_all(sent, axes, 0, 0, tiled=True).reshape(analysed.shape)]
    all_to_all x3 -> x1, starting transfers between devices: 18 us -> 3.74 us  [local(): late = lax.all_to_all(late, axes, 0, 0, tiled=True)]
    all_to_all x3 -> x1, waiting for transfers between devices: 13.4 us -> 0.01 us  [local(): late = lax.all_to_all(late, axes, 0, 0, tiled=True)]
    ppermute x2 -> x4, waiting for transfers between devices: 0.56 us -> 8.56 us  [the longest x3 8.56 us: local(): lax.ppermute(pieces[d], 'zc', [(i, (i + d) % PLANE) for i in range(PLANE)])]
    all_to_all x1, waiting for transfers between devices: 12.7 us -> 9.49 us  [local(): early = lax.all_to_all(early, axes, 0, 0, tiled=True)]
    ppermute x2 -> x4, starting transfers between devices: 5.28 us -> 3.53 us  [the longest x3 2.87 us: local(): lax.ppermute(pieces[d], 'zc', [(i, (i + d) % PLANE) for i in range(PLANE)])]
  transfers between devices with their start and end apart: 12 -> 12, of which waited for: 3 -> 5; matrix products, arithmetic and copies ran while one was open for 0% -> 1% of each run, Pallas kernels for 25% -> 22%
where the time goes in v2:
time: 195 us; the launch traced here: 194 us
  Pallas kernels  99.2 us (51%)
  blocking collectives  38.5 us (20%)
  starting transfers between devices  32 us (16%)
  waiting for transfers between devices  18.2 us (9%)
  local copies, waits for them, and re-layouts  3.66 us (2%)
    pallas_call x3, Pallas kernels, forecast(): pl.pallas_call(forecast_kernel, grid=((end - begin) // 2,), in_specs=[pl....  47.1 us
    all_to_all x1, blocking collectives, local(): back = lax.all_to_all(sent, axes, 0, 0, tiled=True).reshape(analysed.shape)  38.5 us
    pallas_call x2, Pallas kernels, transforms(): pl.pallas_call(partial(transform_kernel, bool(halo)), out_shape=jax.Shape...  15.6 us
    pallas_call x2, Pallas kernels, pack(): pl.pallas_call(partial(pack_kernel, tiles), grid=(1,), in_specs=[pl.Block...  12.6 us
    all_to_all x1, waiting for transfers between devices, local(): early = lax.all_to_all(early, axes, 0, 0, tiled=True)  9.49 us
    all_to_all x1, starting transfers between devices, local(): early = lax.all_to_all(early, axes, 0, 0, tiled=True)  9.42 us
    ppermute x3, waiting for transfers between devices, local(): lax.ppermute(pieces[d], 'zc', [(i, (i + d) % PLANE) for i in range(PLANE)])  8.56 us
    ppermute x2, starting transfers between devices, around(): top = lax.ppermute(cells[PLANE - 1], 'y', downward)  8.01 us
  transfers between devices with their start and end apart: 12, of which 5 were waited for; matrix products, arithmetic and copies ran while one was open for 1% of the time, Pallas kernels for 22%

profile of v2, /device:TPU:1, one launch (start us, length us, event | category | flops | bytes accessed | tf_op | source)
XLA Modules:
  0.0 193.6 jit_solution(10680332518520973275)
XLA Ops:
  0.0 6.3 %pack.3 = bf16[32,9,16,128]{3,2,1,0:T(8,128)(2,1)} custom-call(f32[256,4096]{1,0:T(8,128)} %bitcast.26), custom_call_target="tpu_custom_call" | custom-call | tf_op jit(solution)/shard_map/pack/pallas_call | solution.py:135
  6.3 9.4 %all-to-all-start.1 = ((bf16[32,9,16,128]{3,2,1,0:T(8,128)(2,1)}), bf16[32,9,16,128]{3,2,1,0:T(8,128)(2,1)S(1)}, u32[]{:S(2)}, u32[]{:S(2)}) async-start(bf16[32,9,16,128]{3,2,1,0:T(8,128)(2,1)} %pack.3), calls=%async_computation.1 | async-start | bytes 2359296 | tf_op jit(solution)/shard_map/all_to_all | solution.py:545
  15.7 0.6 pad_add_fusion.me_ref
  16.3 1.9 pack_extra.1
  18.2 0.7 collective-permute-start.2
  18.9 6.3 %pack.2 = bf16[32,9,16,128]{3,2,1,0:T(8,128)(2,1)} custom-call(f32[256,4096]{1,0:T(8,128)} %bitcast.27), custom_call_target="tpu_custom_call" | custom-call | tf_op jit(solution)/shard_map/pack/pallas_call | solution.py:135
  25.2 0.0 copy-start.4
  25.2 9.5 %all-to-all-done.1 = bf16[32,9,16,128]{3,2,1,0:T(8,128)(2,1)S(1)} async-done(((bf16[32,9,16,128]{3,2,1,0:T(8,128)(2,1)}), bf16[32,9,16,128]{3,2,1,0:T(8,128)(2,1)S(1)}, u32[]{:S(2)}, u32[]{:S(2)}) %all-to-all-start.1) | async-done | bytes 1179680 | tf_op jit(solution)/shard_map/all_to_all | solution.py:545
  34.7 0.0 copy-start
  34.7 3.7 %all-to-all-start = ((bf16[32,9,16,128]{3,2,1,0:T(8,128)(2,1)}), bf16[32,9,16,128]{3,2,1,0:T(8,128)(2,1)S(1)}, u32[]{:S(2)}, u32[]{:S(2)}) async-start(bf16[32,9,16,128]{3,2,1,0:T(8,128)(2,1)} %pack.2), calls=%async_computation | async-start | bytes 2359296 | tf_op jit(solution)/shard_map/all_to_all | solution.py:547
  38.5 0.0 copy-done.4
  38.5 0.7 add_convert_fusion.inside
  39.2 0.0 collective-permute-done.2
  39.2 1.7 collective-permute-start.3
  40.9 0.0 copy-done
  40.9 1.3 collective-permute-start.1
  42.2 4.0 %collective-permute-start = (bf16[8,9,16,128]{3,2,1,0:T(8,128)(2,1)S(1)}, bf16[8,9,16,128]{3,2,1,0:T(8,128)(2,1)S(1)}, u32[]{:S(2)}, u32[]{:S(2)}) collective-permute-start(bf16[8,9,16,128]{3,2,1,0:T(8,128)(2,1)S(1)} %get-tuple-element.26), channel_id=1, source_target_pairs={{0,4},{4,8},{8,12},{1,5},{5,9},{9,13},{2,6},{6,10},{10,14},{3,7},{... | collective-permute-start | bytes 884744 | tf_op jit(solution)/shard_map/ppermute | solution.py:552
  46.3 0.1 collective-permute-start.4
  46.4 1.1 collective-permute-start.5
  47.5 0.6 pad_maximum_fusion.own
  48.1 3.4 %collective-permute-done.3.one = f32[16,1024]{1,0:T(8,128)S(1)} collective-permute-done((f32[16,1024]{1,0:T(8,128)S(1)}, f32[16,1024]{1,0:T(8,128)S(1)}, u32[]{:S(2)}, u32[]{:S(2)}) %collective-permute-start.3) | collective-permute-done | bytes 65568 | tf_op jit(solution)/shard_map/ppermute | solution.py:541
  51.5 0.0 copy-start.9
  51.5 4.6 %collective-permute-done.4.two = f32[16,1024]{1,0:T(8,128)S(1)} collective-permute-done((f32[16,1024]{1,0:T(8,128)S(1)}, f32[16,1024]{1,0:T(8,128)S(1)}, u32[]{:S(2)}, u32[]{:S(2)}) %collective-permute-start.4) | collective-permute-done | bytes 65568 | tf_op jit(solution)/shard_map/ppermute | solution.py:541
  56.1 0.0 copy-start.10
  56.1 0.5 collective-permute-done.5.three
  56.6 0.0 copy-done.9
  56.6 0.1 copy-done.10
  56.7 0.0 copy-start.11
  56.7 0.6 copy-done.11
  57.3 1.8 forcing.1
  59.2 0.0 collective-permute-done.1.bottom
  59.2 0.0 copy-start.2
  59.2 0.0 collective-permute-done.top
  59.2 0.0 copy-start.3
  59.2 0.7 copy-done.2
  59.9 0.1 copy-done.3
  60.0 12.2 %forecast.3.refs_0_ = f32[4,64,1024]{2,1,0:T(8,128)} custom-call(f32[2]{0:T(128)} %add_convert_fusion.inside, bf16[4,8,9,16,128]{4,3,2,1,0:T(8,128)(2,1)} %bitcast.28, bf16[8,9,16,128]{3,2,1,0:T(8,128)(2,1)} %copy-done.3, bf16[8,9,16,128]{3,2,1,0:T(8,128)(2,1)} %copy-done.2, f32[3,48,8,128]{3,2,1,0:T(8,128)} %get-tuple-element.16.force), custom_call_target="tpu_custom_call" | custom-call | tf_op jit(solution)/shard_map/forecast/pallas_call | solution.py:250
  72.3 0.0 all-to-all-done
  72.3 0.0 copy-start.1
  72.3 1.3 collective-permute-start.7
  73.6 4.0 %collective-permute-start.6 = (bf16[8,9,16,128]{3,2,1,0:T(8,128)(2,1)S(1)}, bf16[8,9,16,128]{3,2,1,0:T(8,128)(2,1)S(1)}, u32[]{:S(2)}, u32[]{:S(2)}) collective-permute-start(bf16[8,9,16,128]{3,2,1,0:T(8,128)(2,1)S(1)} %get-tuple-element.24), channel_id=1, source_target_pairs={{0,4},{4,8},{8,12},{1,5},{5,9},{9,13},{2,6},{6,10},{10,14},{3,7},{... | collective-permute-start | bytes 884744 | tf_op jit(solution)/shard_map/ppermute | solution.py:552
  77.6 12.3 %forecast.4.refs_1_ = f32[4,64,1024]{2,1,0:T(8,128)} custom-call(f32[2]{0:T(128)} %add_convert_fusion.inside, bf16[4,8,9,16,128]{4,3,2,1,0:T(8,128)(2,1)} %bitcast.29, bf16[8,9,16,128]{3,2,1,0:T(8,128)(2,1)} %copy-done.3, bf16[8,9,16,128]{3,2,1,0:T(8,128)(2,1)} %copy-done.2, f32[3,48,8,128]{3,2,1,0:T(8,128)} %get-tuple-element.16.force), custom_call_target="tpu_custom_call" | custom-call | tf_op jit(solution)/shard_map/forecast/pallas_call | solution.py:250
  89.9 0.0 copy-done.1
  89.9 0.0 collective-permute-done.7.bottom
  89.9 0.0 copy-start.5
  89.9 0.0 collective-permute-done.6.top
  90.0 0.0 copy-start.6
  90.0 0.7 copy-done.5
  90.6 0.1 copy-done.6
  90.7 22.6 %forecast.5.refs_2_ = f32[4,128,1024]{2,1,0:T(8,128)} custom-call(f32[2]{0:T(128)} %add_convert_fusion.inside, bf16[4,8,9,16,128]{4,3,2,1,0:T(8,128)(2,1)} %bitcast.32, bf16[8,9,16,128]{3,2,1,0:T(8,128)(2,1)} %copy-done.6, bf16[8,9,16,128]{3,2,1,0:T(8,128)(2,1)} %copy-done.5, f32[3,48,8,128]{3,2,1,0:T(8,128)} %get-tuple-element.16.force), custom_call_target="tpu_custom_call" | custom-call | tf_op jit(solution)/shard_map/forecast/pallas_call | solution.py:250
  113.3 7.6 %curvature.1 = (f32[4,264,256]{2,1,0:T(8,128)}, f32[264,256]{1,0:T(8,128)}, f32[264,256]{1,0:T(8,128)}) custom-call(f32[4,64,1024]{2,1,0:T(8,128)} %forecast.3.refs_0_, f32[4,64,1024]{2,1,0:T(8,128)} %forecast.4.refs_1_, f32[4,128,1024]{2,1,0:T(8,128)} %forecast.5.refs_2_, f32[4,8,1024]{2,1,0:T(8,128)} %get-tuple-element.19.refs_3_), custom_call_target="tpu_custom_call" | custom-call | tf_op jit(solution)/shard_map/curvature/pallas_call | solution.py:364
  120.9 3.2 %collective-permute-start.8 = (f32[264,256]{1,0:T(8,128)}, f32[264,256]{1,0:T(8,128)S(1)}, u32[]{:S(2)}, u32[]{:S(2)}) collective-permute-start(f32[264,256]{1,0:T(8,128)} %get-tuple-element.21), channel_id=1, source_target_pairs={{0,4},{4,8},{8,12},{1,5},{5,9},{9,13},{2,6},{6,10},{10,14},{3,7},{... | collective-permute-start | bytes 811016 | tf_op jit(solution)/shard_map/ppermute | solution.py:564
  124.1 1.5 collective-permute-start.9
  125.6 7.8 %transform.2.refs_3_ = f32[2,264,256]{2,1,0:T(8,128)} custom-call(f32[4,264,256]{2,1,0:T(8,128)} %get-tuple-element.20.refs_0_), custom_call_target="tpu_custom_call" | custom-call | tf_op jit(solution)/shard_map/transform/pallas_call | solution.py:431
  133.3 0.0 collective-permute-done.8.refs_1_
  133.3 0.0 copy-start.7
  133.3 0.1 collective-permute-done.9.refs_2_
  133.5 0.5 copy-done.7
  134.0 0.0 copy-start.8
  134.0 0.7 copy-done.8
  134.7 7.9 %transform.3.refs_4_ = f32[2,264,256]{2,1,0:T(8,128)} custom-call(f32[4,264,256]{2,1,0:T(8,128)} %get-tuple-element.20.refs_0_, f32[264,256]{1,0:T(8,128)} %copy-done.7, f32[264,256]{1,0:T(8,128)} %copy-done.8), custom_call_target="tpu_custom_call" | custom-call | tf_op jit(solution)/shard_map/transform/pallas_call | solution.py:431
  142.6 5.9 %apply.1 = bf16[4,8,272,128]{3,2,1,0:T(8,128)(2,1)} custom-call(f32[4,64,1024]{2,1,0:T(8,128)} %forecast.3.refs_0_, f32[4,64,1024]{2,1,0:T(8,128)} %forecast.4.refs_1_, f32[4,128,1024]{2,1,0:T(8,128)} %forecast.5.refs_2_, f32[2,264,256]{2,1,0:T(8,128)} %transform.2.refs_3_, f32[2,264,256]{2,1,0:T(8,128)} %transform.3.refs_4_), custom_call_target="tpu_custom_call" | custom-call | tf_op jit(solution)/shard_map/apply/pallas_call | solution.py:472
  148.5 38.5 %all_to_all.15 = bf16[32,272,128]{2,1,0:T(8,128)(2,1)} all-to-all(bf16[32,272,128]{2,1,0:T(8,128)(2,1)} %bitcast.30), channel_id=1, replica_groups=mesh['member'=8,'y'=4,'zc'=4] {'zc','member'}, dimensions={0} | all-to-all | bytes 4456448 | tf_op jit(solution)/shard_map/all_to_all | solution.py:569
  187.0 6.6 %unpack.1 = f32[256,4096]{1,0:T(8,128)} custom-call(bf16[4,8,272,128]{3,2,1,0:T(8,128)(2,1)} %bitcast.31), custom_call_target="tpu_custom_call" | custom-call | tf_op jit(solution)/shard_map/unpack/pallas_call | solution.py:509
  (7 shorter events, 0.1 us)
Async XLA Ops:
  6.3 28.4 %all-to-all-start.1 = ((bf16[32,9,16,128]{3,2,1,0:T(8,128)(2,1)}), bf16[32,9,16,128]{3,2,1,0:T(8,128)(2,1)S(1)}, u32[]{:S(2)}, u32[]{:S(2)}) async-start(bf16[32,9,16,128]{3,2,1,0:T(8,128)(2,1)} %pack.3), calls=%async_computation.1 | async-start | bytes 2359296 | tf_op jit(solution)/shard_map/all_to_all | solution.py:545
  18.2 20.9 %collective-permute-start.2 = (f32[4,8,1024]{2,1,0:T(8,128)}, f32[4,8,1024]{2,1,0:T(8,128)S(1)}, u32[]{:S(2)}, u32[]{:S(2)}) collective-permute-start(f32[4,8,1024]{2,1,0:T(8,128)} %pack_extra.1), channel_id=1, source_target_pairs={{4,0},{8,4},{12,8},{3,7},{7,11},{11,15},{20,16},{24,20},{28,24},{1... | collective-permute-start | bytes 393224 | tf_op jit(solution)/shard_map/ppermute | solution.py:538
  25.2 13.3 %copy-start.4 = (f32[4,8,1024]{2,1,0:T(8,128)S(1)}, f32[4,8,1024]{2,1,0:T(8,128)}, u32[]{:S(2)}) copy-start(f32[4,8,1024]{2,1,0:T(8,128)} %pack_extra.1) | copy-start | bytes 393220
  34.7 6.2 %copy-start = (bf16[32,9,16,128]{3,2,1,0:T(8,128)(2,1)}, bf16[32,9,16,128]{3,2,1,0:T(8,128)(2,1)S(1)}, u32[]{:S(2)}) copy-start(bf16[32,9,16,128]{3,2,1,0:T(8,128)(2,1)S(1)} %all-to-all-done.1) | copy-start | bytes 3538948
  34.7 37.5 %all-to-all-start = ((bf16[32,9,16,128]{3,2,1,0:T(8,128)(2,1)}), bf16[32,9,16,128]{3,2,1,0:T(8,128)(2,1)S(1)}, u32[]{:S(2)}, u32[]{:S(2)}) async-start(bf16[32,9,16,128]{3,2,1,0:T(8,128)(2,1)} %pack.2), calls=%async_computation | async-start | bytes 2359296 | tf_op jit(solution)/shard_map/all_to_all | solution.py:547
  39.2 12.3 %collective-permute-start.3 = (f32[16,1024]{1,0:T(8,128)S(1)}, f32[16,1024]{1,0:T(8,128)S(1)}, u32[]{:S(2)}, u32[]{:S(2)}) collective-permute-start(f32[16,1024]{1,0:T(8,128)S(1)} %pad_maximum_fusion.1), channel_id=1, source_target_pairs={{0,1},{1,2},{2,3},{3,0},{4,5},{5,6},{6,7},{7,4},{8,9},{9,10},{10,1... | collective-permute-start | bytes 196616 | tf_op jit(solution)/shard_map/ppermute | solution.py:541
  40.9 18.3 %collective-permute-start.1 = (bf16[8,9,16,128]{3,2,1,0:T(8,128)(2,1)S(1)}, bf16[8,9,16,128]{3,2,1,0:T(8,128)(2,1)S(1)}, u32[]{:S(2)}, u32[]{:S(2)}) collective-permute-start(bf16[8,9,16,128]{3,2,1,0:T(8,128)(2,1)S(1)} %get-tuple-element.25), channel_id=1, source_target_pairs={{4,0},{8,4},{12,8},{5,1},{9,5},{13,9},{6,2},{10,6},{14,10},{7,3},{... | collective-permute-start | bytes 884744 | tf_op jit(solution)/shard_map/ppermute | solution.py:551
  42.2 17.0 %collective-permute-start = (bf16[8,9,16,128]{3,2,1,0:T(8,128)(2,1)S(1)}, bf16[8,9,16,128]{3,2,1,0:T(8,128)(2,1)S(1)}, u32[]{:S(2)}, u32[]{:S(2)}) collective-permute-start(bf16[8,9,16,128]{3,2,1,0:T(8,128)(2,1)S(1)} %get-tuple-element.26), channel_id=1, source_target_pairs={{0,4},{4,8},{8,12},{1,5},{5,9},{9,13},{2,6},{6,10},{10,14},{3,7},{... | collective-permute-start | bytes 884744 | tf_op jit(solution)/shard_map/ppermute | solution.py:552
  46.3 9.8 %collective-permute-start.4 = (f32[16,1024]{1,0:T(8,128)S(1)}, f32[16,1024]{1,0:T(8,128)S(1)}, u32[]{:S(2)}, u32[]{:S(2)}) collective-permute-start(f32[16,1024]{1,0:T(8,128)S(1)} %pad_maximum_fusion.2), channel_id=1, source_target_pairs={{0,2},{1,3},{2,0},{3,1},{4,6},{5,7},{6,4},{7,5},{8,10},{9,11},{10,... | collective-permute-start | bytes 196616 | tf_op jit(solution)/shard_map/ppermute | solution.py:541
  46.4 10.3 %collective-permute-start.5 = (f32[16,1024]{1,0:T(8,128)S(1)}, f32[16,1024]{1,0:T(8,128)S(1)}, u32[]{:S(2)}, u32[]{:S(2)}) collective-permute-start(f32[16,1024]{1,0:T(8,128)S(1)} %pad_maximum_fusion.3), channel_id=1, source_target_pairs={{0,3},{1,0},{2,1},{3,2},{4,7},{5,4},{6,5},{7,6},{8,11},{9,8},{10,9... | collective-permute-start | bytes 196616 | tf_op jit(solution)/shard_map/ppermute | solution.py:541
  51.5 5.1 %copy-start.9 = (f32[16,1024]{1,0:T(8,128)}, f32[16,1024]{1,0:T(8,128)S(1)}, u32[]{:S(2)}) copy-start(f32[16,1024]{1,0:T(8,128)S(1)} %collective-permute-done.3.one) | copy-start | bytes 196612
  56.1 0.6 copy-start.10
  56.7 0.6 copy-start.11
  59.2 0.7 copy-start.2
  59.2 0.8 copy-start.3
  72.3 17.7 %copy-start.1 = (bf16[32,9,16,128]{3,2,1,0:T(8,128)(2,1)}, bf16[32,9,16,128]{3,2,1,0:T(8,128)(2,1)S(1)}, u32[]{:S(2)}) copy-start(bf16[32,9,16,128]{3,2,1,0:T(8,128)(2,1)S(1)} %all-to-all-done) | copy-start | bytes 3538948
  72.3 17.6 %collective-permute-start.7 = (bf16[8,9,16,128]{3,2,1,0:T(8,128)(2,1)S(1)}, bf16[8,9,16,128]{3,2,1,0:T(8,128)(2,1)S(1)}, u32[]{:S(2)}, u32[]{:S(2)}) collective-permute-start(bf16[8,9,16,128]{3,2,1,0:T(8,128)(2,1)S(1)} %get-tuple-element.23), channel_id=1, source_target_pairs={{4,0},{8,4},{12,8},{5,1},{9,5},{13,9},{6,2},{10,6},{14,10},{7,3},{... | collective-permute-start | bytes 884744 | tf_op jit(solution)/shard_map/ppermute | solution.py:551
  73.6 16.3 %collective-permute-start.6 = (bf16[8,9,16,128]{3,2,1,0:T(8,128)(2,1)S(1)}, bf16[8,9,16,128]{3,2,1,0:T(8,128)(2,1)S(1)}, u32[]{:S(2)}, u32[]{:S(2)}) collective-permute-start(bf16[8,9,16,128]{3,2,1,0:T(8,128)(2,1)S(1)} %get-tuple-element.24), channel_id=1, source_target_pairs={{0,4},{4,8},{8,12},{1,5},{5,9},{9,13},{2,6},{6,10},{10,14},{3,7},{... | collective-permute-start | bytes 884744 | tf_op jit(solution)/shard_map/ppermute | solution.py:552
  89.9 0.7 copy-start.5
  90.0 0.8 copy-start.6
  120.9 12.4 %collective-permute-start.8 = (f32[264,256]{1,0:T(8,128)}, f32[264,256]{1,0:T(8,128)S(1)}, u32[]{:S(2)}, u32[]{:S(2)}) collective-permute-start(f32[264,256]{1,0:T(8,128)} %get-tuple-element.21), channel_id=1, source_target_pairs={{0,4},{4,8},{8,12},{1,5},{5,9},{9,13},{2,6},{6,10},{10,14},{3,7},{... | collective-permute-start | bytes 811016 | tf_op jit(solution)/shard_map/ppermute | solution.py:564
  124.1 9.4 %collective-permute-start.9 = (f32[264,256]{1,0:T(8,128)}, f32[264,256]{1,0:T(8,128)S(1)}, u32[]{:S(2)}, u32[]{:S(2)}) collective-permute-start(f32[264,256]{1,0:T(8,128)} %get-tuple-element.22), channel_id=1, source_target_pairs={{4,0},{8,4},{12,8},{5,1},{9,5},{13,9},{6,2},{10,6},{14,10},{7,3},{... | collective-permute-start | bytes 811016 | tf_op jit(solution)/shard_map/ppermute | solution.py:563
  133.3 0.7 copy-start.7
  134.0 0.7 copy-start.8
